TPU v7x, 32 devices: a whole 2x2x4 slice. The times are simulated.
32 devices in a mesh: seq: 16 (over z, y, x), dp: 2 (over core).
Axes of the slice: x: 2, y: 2, z: 4, core: 2. Of those that a mesh axis runs over, the one named last changes fastest.
Arguments:
- clip: bfloat16 [16, 128, 1152], P('seq'), may hold values from -40 to 40
- offsets: bfloat16 [2, 16, 128, 1152], P('dp', 'seq'), may hold values from -6 to 6
- cotangent: bfloat16 [2, 16, 128, 1152], P('dp', 'seq'), may hold values from -6 to 6
- gain_time: float32 [1152], replicated, may hold values from 0.1 to 1.9
- gain_space: float32 [1152], replicated, may hold values from 0.1 to 1.9
- proj_time: bfloat16 [1152, 1728], P('dp'), may hold values from -0.1875 to 0.1875
- out_time: bfloat16 [576, 1152], P('dp'), may hold values from -0.25 to 0.25
- proj_space: bfloat16 [1152, 1728], P('dp'), may hold values from -0.1875 to 0.1875
- out_space: bfloat16 [576, 1152], P('dp'), may hold values from -0.25 to 0.25
- bias_time: float32 [8, 16, 16], replicated, may hold values from -3 to 303
- bias_space: float32 [8, 128, 128], P(None, 'dp'), may hold values from -3 to 303
Outputs:
- clip_grad: float32 [16, 128, 1152], P('seq', 'dp')
All inputs are finite; a program needn't handle non-finite values.
Results may differ from a plain program's by a relative error of at most 0.015.
Values may be sent and summed in bfloat16 or wider, within the bound.
A program may use at most 64 MiB of HBM per device.

v0:
```python
import functools
import math

import jax
import jax.numpy as jnp
from jax import lax
from jax.experimental import pallas as pl
from jax.experimental.pallas import tpu as pltpu
from jax.sharding import PartitionSpec as P

HEADS = 8
HD = 72


epsilon = 1e-06


def rms_norm(hidden_in, gain_vec):
    inv_rms = lax.rsqrt(jnp.mean(hidden_in * hidden_in, axis=-1, keepdims=True) + epsilon)
    return ((hidden_in * inv_rms * gain_vec).astype(jnp.bfloat16), inv_rms)


def norm_back(hidden_in, inv_rms, gain_vec, grad_normed):
    weighted = grad_normed.astype(jnp.float32) * gain_vec
    cubed = inv_rms * inv_rms * inv_rms
    return inv_rms * weighted - hidden_in * cubed * jnp.mean(
        weighted * hidden_in, axis=-1, keepdims=True
    )


def layout_forms(frame_major):
    if frame_major:
        return ("lbhe", "mbhe")
    return ("blhe", "bmhe")


def attend(queries, key_rows, values, score_bias, frame_major):
    query_form, key_form = layout_forms(frame_major)
    scaling = 1.0 / math.sqrt(queries.shape[-1])
    scores = (
        jnp.einsum(
            query_form + "," + key_form + "->bhlm",
            queries,
            key_rows,
            preferred_element_type=jnp.float32,
        )
        * scaling
        + score_bias
    )
    highest = jnp.max(scores, axis=-1, keepdims=True)
    exp_scores = jnp.exp(scores - highest)
    probabilities = exp_scores / jnp.sum(exp_scores, axis=-1, keepdims=True)
    context = jnp.einsum(
        "bhlm," + key_form + "->" + query_form,
        probabilities.astype(jnp.bfloat16),
        values,
        preferred_element_type=jnp.float32,
    )
    return (context.astype(jnp.bfloat16), probabilities)


def attend_back(queries, key_rows, values, probabilities, grad_context, frame_major):
    query_form, key_form = layout_forms(frame_major)
    scaling = 1.0 / math.sqrt(queries.shape[-1])
    rounded = probabilities.astype(jnp.bfloat16)
    grad_values = jnp.einsum(
        "bhlm," + query_form + "->" + key_form,
        rounded,
        grad_context,
        preferred_element_type=jnp.float32,
    ).astype(jnp.bfloat16)
    grad_probs = jnp.einsum(
        query_form + "," + key_form + "->bhlm",
        grad_context,
        values,
        preferred_element_type=jnp.float32,
    )
    row_sums = jnp.sum(grad_probs * probabilities, axis=-1, keepdims=True)
    grad_scores = (probabilities * (grad_probs - row_sums) * scaling).astype(jnp.bfloat16)
    grad_queries = jnp.einsum(
        "bhlm," + key_form + "->" + query_form,
        grad_scores,
        key_rows,
        preferred_element_type=jnp.float32,
    ).astype(jnp.bfloat16)
    grad_keys = jnp.einsum(
        "bhlm," + query_form + "->" + key_form,
        grad_scores,
        queries,
        preferred_element_type=jnp.float32,
    ).astype(jnp.bfloat16)
    return (grad_queries, grad_keys, grad_values)


def times_transposed(left, weight):
    return lax.dot_general(
        left, weight, (((1,), (1,)), ((), ())), preferred_element_type=jnp.float32
    )


def regroup(arranged):
    return lax.all_to_all(arranged, "seq", split_axis=0, concat_axis=1, tiled=True)


def to_positions(matrix, stack_count):
    seq_count = lax.axis_size("seq")
    local_rows = matrix.shape[0] // seq_count
    col_count = matrix.shape[1] // stack_count
    arranged = matrix.reshape(seq_count, 1, local_rows, stack_count, col_count)
    return regroup(arranged)[0]


def to_frames(arranged):
    seq_count = lax.axis_size("seq")
    frame_count, local_rows, stack_count, col_count = arranged.shape
    returned = regroup(arranged.reshape(frame_count, 1, local_rows, stack_count, col_count))
    return returned.reshape(seq_count * local_rows, stack_count * col_count)


def per_device(
    clip,
    offsets,
    cotangent,
    gain_time,
    gain_space,
    proj_time,
    out_time,
    proj_space,
    out_space,
    bias_time,
    bias_space,
):
    proj_time, out_time, proj_space, out_space = (
        lax.all_gather(proj_time, "dp", axis=0, tiled=True),
        lax.all_gather(out_time, "dp", axis=0, tiled=True),
        lax.all_gather(proj_space, "dp", axis=0, tiled=True),
        lax.all_gather(out_space, "dp", axis=0, tiled=True),
    )
    bias_space = lax.all_gather(bias_space, "dp", axis=1, tiled=True)
    seq_count = lax.axis_size("seq")
    pos_count = clip.shape[1]
    local_rows = pos_count // seq_count
    head_cols = HEADS * HD
    hidden_in = clip[0].astype(jnp.float32) + offsets[0, 0].astype(jnp.float32)
    normed, inv_rms = rms_norm(hidden_in, gain_time)
    arranged_in = to_positions(normed, 1)
    flat_in = arranged_in.reshape(seq_count * local_rows, arranged_in.shape[-1])
    arranged = jnp.dot(flat_in, proj_time, preferred_element_type=jnp.float32).astype(jnp.bfloat16)
    arranged = arranged.reshape(seq_count, local_rows, 3, HEADS, HD)
    queries, key_rows, values = (arranged[:, :, 0], arranged[:, :, 1], arranged[:, :, 2])
    context, weights_time = attend(queries, key_rows, values, bias_time, True)
    context_frames = to_frames(context.reshape(seq_count, local_rows, 1, head_cols))
    after_time = hidden_in + jnp.dot(context_frames, out_time, preferred_element_type=jnp.float32)
    normed_space, inv_rms_space = rms_norm(after_time, gain_space)
    stacked_space = jnp.dot(normed_space, proj_space, preferred_element_type=jnp.float32).astype(
        jnp.bfloat16
    )
    stacked_space = stacked_space.reshape(1, pos_count, 3, HEADS, HD)
    queries_space, keys_space, values_space = (
        stacked_space[:, :, 0],
        stacked_space[:, :, 1],
        stacked_space[:, :, 2],
    )
    unused_context, weights_space = attend(
        queries_space, keys_space, values_space, bias_space, False
    )
    grad_out = cotangent[0, 0]
    grad_context = (
        times_transposed(grad_out, out_space).astype(jnp.bfloat16).reshape(1, pos_count, HEADS, HD)
    )
    grads_space = attend_back(
        queries_space, keys_space, values_space, weights_space, grad_context, False
    )
    grad_normed = times_transposed(
        jnp.stack(grads_space, axis=2).reshape(pos_count, 3 * head_cols), proj_space
    ).astype(jnp.bfloat16)
    grad_after = grad_out.astype(jnp.float32) + norm_back(
        after_time, inv_rms_space, gain_space, grad_normed
    )
    grad_context_time = times_transposed(grad_after.astype(jnp.bfloat16), out_time).astype(
        jnp.bfloat16
    )
    grad_context_pos = to_positions(grad_context_time, 1).reshape(seq_count, local_rows, HEADS, HD)
    grads_time = attend_back(queries, key_rows, values, weights_time, grad_context_pos, True)
    stacked_grads = jnp.stack(grads_time, axis=2)
    grad_pos = times_transposed(
        stacked_grads.reshape(seq_count * local_rows, 3 * head_cols), proj_time
    ).astype(jnp.bfloat16)
    grad_normed_time = to_frames(grad_pos.reshape(seq_count, local_rows, 1, grad_pos.shape[-1]))
    grad_in = grad_after + norm_back(hidden_in, inv_rms, gain_time, grad_normed_time)
    summed = lax.psum_scatter(
        grad_in.astype(jnp.bfloat16), "dp", scatter_dimension=0, tiled=True
    ).astype(jnp.float32)
    return summed[None]


LANES = 128
MASKED = -1e30


def dot_nn(left, right):
    return lax.dot_general(left, right, (((1,), (0,)), ((), ())), preferred_element_type=jnp.float32)


def dot_nt(left, right):
    return lax.dot_general(left, right, (((1,), (1,)), ((), ())), preferred_element_type=jnp.float32)


def dot_tn(left, right):
    return lax.dot_general(left, right, (((0,), (0,)), ((), ())), preferred_element_type=jnp.float32)


def head_window(head):
    low, high = head * HD, (head + 1) * HD
    first = low // LANES * LANES
    last = -(-high // LANES) * LANES
    lane = lax.broadcasted_iota(jnp.int32, (1, last - first), 1) + first
    return first, last, (lane >= low) & (lane < high)


def add_tiles(tiles, first, block):
    for col in range(0, block.shape[1], LANES):
        tile = (first + col) // LANES
        piece = block[:, col : col + LANES]
        tiles[tile] = piece if tiles[tile] is None else tiles[tile] + piece


def softmax(scores):
    exp_scores = jnp.exp(scores - jnp.max(scores, axis=-1, keepdims=True))
    return exp_scores * (1.0 / jnp.sum(exp_scores, axis=-1, keepdims=True))


def fused_kernel(
    seq_count,
    clip_in,
    off_in,
    cot_in,
    gain_time_in,
    gain_space_in,
    bias_time_in,
    proj_time_in,
    out_time_in,
    proj_space_in,
    out_space_in,
    bias_space_in,
    out_ref,
    clip_ref,
    off_ref,
    cot_ref,
    gain_time_ref,
    gain_space_ref,
    bias_time_ref,
    proj_time_t,
    out_time_t,
    proj_space_t,
    proj_time,
    out_time,
    proj_space,
    out_space,
    bias_space,
    bias_wide,
    hidden,
    after,
    q_time,
    k_time,
    v_time,
    probs_time,
    stacked,
    dc_space,
    dc_time,
    send_normed,
    got_normed,
    send_ctx,
    got_ctx,
    send_dc,
    got_dc,
    totals,
    pair_send,
    pair_got,
    send_back,
    got_back,
    after_send,
    after_got,
    send_sems,
    recv_sems,
    back_send_sems,
    back_recv_sems,
    weight_sems,
    weight_send_sems,
    weight_recv_sems,
    pair_send_sems,
    pair_recv_sems,
    input_sems,
):
    me = lax.axis_index("seq")
    core = lax.axis_index("dp")
    other = 1 - core
    tokens, width = hidden.shape
    rows = tokens // seq_count
    half = tokens // 2
    half_blocks = seq_count // 2
    wide = q_time.shape[1]
    scaling = 1.0 / math.sqrt(HD)

    barrier = pltpu.get_barrier_semaphore()
    for step in range(seq_count):
        peer = lax.rem(me + step, seq_count)
        if step:
            pl.semaphore_signal(
                barrier, inc=1, device_id=(peer, core), device_id_type=pl.DeviceIdType.MESH
            )
        pl.semaphore_signal(
            barrier, inc=1, device_id=(peer, other), device_id_type=pl.DeviceIdType.MESH
        )

    inputs = (clip_in, off_in, gain_time_in, bias_time_in, cot_in, gain_space_in)
    places = (clip_ref, off_ref, gain_time_ref, bias_time_ref, cot_ref, gain_space_ref)
    input_copies = [
        pltpu.make_async_copy(source, target, input_sems.at[place])
        for place, (source, target) in enumerate(zip(inputs, places))
    ]
    for copy in input_copies:
        copy.start()

    sources = (out_space_in, proj_time_in, out_time_in, proj_space_in)
    targets = (out_space, proj_time, out_time, proj_space)

    def part(place):
        if place == len(sources):
            count = bias_space_in.shape[1]
            start = pl.multiple_of(core * count, count)
            return bias_space_in, bias_space.at[:, pl.ds(start, count)]
        count = sources[place].shape[0]
        start = pl.multiple_of(core * count, count)
        return sources[place], targets[place].at[pl.ds(start, count)]

    weight_count = len(sources) + 1
    own_copies, pair_copies = [], []
    for place in range(weight_count):
        source, target = part(place)
        own_copies.append(pltpu.make_async_copy(source, target, weight_sems.at[place]))
        pair_copies.append(
            pltpu.make_async_remote_copy(
                src_ref=source,
                dst_ref=target,
                send_sem=weight_send_sems.at[place],
                recv_sem=weight_recv_sems.at[place],
                device_id=(me, other),
                device_id_type=pl.DeviceIdType.MESH,
            )
        )
        own_copies[-1].start()

    def weight_ready(place):
        own_copies[place].wait()
        pair_copies[place].wait_recv()

    def partner(step):
        place, bit = me, 1
        while bit <= step:
            if step & bit:
                place = place + bit * (1 - 2 * (me // bit % 2))
            bit *= 2
        return place

    def exchange(phase, sent, got, first, last):
        columns = pl.ds(first, last - first)

        def message(step, landing):
            target = partner(step)
            return pltpu.make_async_remote_copy(
                src_ref=sent.at[target, :, columns],
                dst_ref=got.at[landing(target), :, columns],
                send_sem=send_sems.at[phase, step],
                recv_sem=recv_sems.at[phase, step],
                device_id=(target, core),
                device_id_type=pl.DeviceIdType.MESH,
            )

        def start():
            for step in range(seq_count - 1, 0, -1):
                message(step, lambda target: me).start()
            got[me, :, first:last] = sent[me, :, first:last]

        def arrive():
            for step in range(seq_count - 1, 0, -1):
                message(step, lambda target: target).wait_recv()

        def finish():
            for step in range(1, seq_count):
                message(step, lambda target: me).wait_send()

        return start, arrive, finish

    def merged(ref, first=0, last=None):
        last = ref.shape[-1] if last is None else last
        block = ref[:, :, first:last].astype(jnp.float32)
        return block.reshape(tokens, last - first)

    def split(value):
        return value.reshape(seq_count, rows, value.shape[-1]).astype(jnp.bfloat16)

    def gain_row(gain_ref):
        pieces = [gain_ref[place : place + 1, :] for place in range(gain_ref.shape[0])]
        return jnp.concatenate(pieces, axis=1)

    def norm(value, gain_ref):
        inv_rms = lax.rsqrt(jnp.mean(value * value, axis=-1, keepdims=True) + epsilon)
        return value * inv_rms * gain_row(gain_ref), inv_rms

    def project(chunks, weight):
        head_cols = HEADS * HD
        whole = head_cols // LANES * LANES
        cuts = ((0, whole), (whole, 2 * head_cols), (2 * head_cols, 3 * head_cols))
        sums = None
        for first, last, give in chunks:
            block = give()
            terms = [dot_nn(block, weight[first:last, low:high]) for low, high in cuts]
            sums = terms if sums is None else [a + b for a, b in zip(sums, terms)]
        left, middle, values = sums
        queries = jnp.concatenate([left, middle[:, :LANES]], axis=1)
        key_rows = pltpu.roll(middle, middle.shape[1] - (head_cols - whole), 1)
        return queries.astype(jnp.bfloat16), key_rows.astype(jnp.bfloat16), values.astype(jnp.bfloat16)

    def stack_grads(dq, dk, dv):
        head_cols = HEADS * HD
        whole = head_cols // LANES * LANES
        count = len(dq)
        dq = jnp.concatenate(dq, axis=1)
        dk = pltpu.roll(jnp.concatenate(dk, axis=1), head_cols - whole, 1)
        dv = jnp.concatenate(dv, axis=1)
        stacked[:, :whole] = dq[:, :whole].astype(jnp.bfloat16)
        stacked[:, whole : whole + LANES] = (dq[:, whole:] + dk[:, :LANES]).astype(jnp.bfloat16)
        stacked[:, whole + LANES : 2 * head_cols] = dk[:, LANES:].astype(jnp.bfloat16)
        stacked[:, 2 * head_cols :] = dv[:, :head_cols].astype(jnp.bfloat16)

    def own(mask, block):
        return jnp.where(mask, block, jnp.zeros_like(block))

    def back_one(head, queries, key_rows, values, probs, grad_ctx, sums):
        first, last, mask = head_window(head)
        dq, dk, dv = sums
        query, key, value, dc = (
            ref[:, first:last] for ref in (queries, key_rows, values, grad_ctx)
        )
        add_tiles(dv, first, dot_tn(probs.astype(jnp.bfloat16), own(mask, dc)))
        dw = dot_nt(dc, own(mask, value))
        mean_dw = jnp.sum(dw * probs, axis=-1, keepdims=True)
        ds = (probs * (dw - mean_dw) * scaling).astype(jnp.bfloat16)
        add_tiles(dq, first, dot_nn(ds, own(mask, key)))
        add_tiles(dk, first, dot_tn(ds, own(mask, query)))

    def turn(weight, turned):
        for first in range(0, weight.shape[0], LANES):
            turned[:, first : first + LANES] = weight[first : first + LANES, :].T

    tile_count = wide // LANES

    for copy in input_copies:
        copy.wait()
    hidden[...] = clip_ref[...].astype(jnp.float32) + off_ref[...].astype(jnp.float32)
    normed, inv_time = norm(hidden[...], gain_time_ref)
    send_normed[...] = split(normed)
    pl.semaphore_wait(barrier, 2 * seq_count - 1)
    feature_cuts = [*range(0, width, 4 * LANES), width]
    chunk_count = len(feature_cuts) - 1
    normed_moves = [
        exchange(place, send_normed, got_normed, feature_cuts[place], feature_cuts[place + 1])
        for place in range(chunk_count)
    ]
    for start, _, _ in normed_moves:
        start()
    for copy in pair_copies:
        copy.start()

    extra = wide - HEADS * HD
    for ref in (out_time, out_space):
        ref[pl.ds(HEADS * HD, extra), :] = jnp.zeros((extra, width), jnp.bfloat16)
    frame = lax.broadcasted_iota(jnp.int32, (seq_count, tokens), 0)
    column = lax.broadcasted_iota(jnp.int32, (seq_count, tokens), 1)
    spread = jnp.where(column // rows == frame, 1.0, 0.0).astype(jnp.float32)
    bias_cols = lax.dot_general(
        bias_time_ref[...],
        spread,
        (((1,), (0,)), ((), ())),
        precision=lax.Precision.HIGHEST,
        preferred_element_type=jnp.float32,
    )
    same = lax.broadcasted_iota(jnp.int32, (tokens, tokens), 0) % rows == (
        lax.broadcasted_iota(jnp.int32, (tokens, tokens), 1) % rows
    )
    for head in range(HEADS):
        block = bias_cols[head * seq_count : (head + 1) * seq_count]
        block = jnp.broadcast_to(block[:, None, :], (seq_count, rows, tokens))
        bias_wide[head] = jnp.where(same, block.reshape(tokens, tokens), MASKED)

    weight_ready(0)
    dc_space[...] = dot_nt(cot_ref[...], out_space[...]).astype(jnp.bfloat16)

    weight_ready(1)
    turn(proj_time, proj_time_t)

    def arrived(place):
        normed_moves[place][1]()
        return merged(got_normed, feature_cuts[place], feature_cuts[place + 1]).astype(jnp.bfloat16)

    queries, key_rows, values = project(
        [
            (feature_cuts[place], feature_cuts[place + 1], functools.partial(arrived, place))
            for place in range(chunk_count)
        ],
        proj_time,
    )
    q_time[...] = queries
    k_time[...] = key_rows
    v_time[:, : HEADS * HD] = values
    ctx = [None] * tile_count
    cut = 2 * LANES
    heads_first = -(-cut // HD)
    ctx_moves = [
        exchange(chunk_count, send_ctx, got_ctx, 0, cut),
        exchange(chunk_count + 1, send_ctx, got_ctx, cut, wide),
    ]
    for head in range(HEADS):
        first, last, mask = head_window(head)
        scores = dot_nt(q_time[:, first:last], own(mask, k_time[:, first:last]))
        probs = softmax(scores * scaling + bias_wide[head])
        probs_time[head] = probs
        add_tiles(ctx, first, dot_nn(probs.astype(jnp.bfloat16), own(mask, v_time[:, first:last])))
        if head == heads_first - 1:
            send_ctx[:, :, :cut] = split(jnp.concatenate(ctx[: cut // LANES], axis=1))
            ctx_moves[0][0]()
    send_ctx[:, :, cut:] = split(jnp.concatenate(ctx[cut // LANES :], axis=1))
    ctx_moves[1][0]()
    weight_ready(2)
    weight_ready(3)
    weight_ready(4)
    turn(proj_space, proj_space_t)
    turn(out_time, out_time_t)
    ctx_moves[0][1]()
    first_part = dot_nn(merged(got_ctx, 0, cut).astype(jnp.bfloat16), out_time[:cut])
    ctx_moves[1][1]()

    second_part = dot_nn(merged(got_ctx, cut, wide).astype(jnp.bfloat16), out_time[cut:])
    after[...] = hidden[...] + (first_part + second_part)
    normed, inv_space = norm(after[...], gain_space_ref)
    queries, key_rows, values = project(
        [(0, width, lambda: normed.astype(jnp.bfloat16))], proj_space
    )
    values = jnp.concatenate([values, jnp.zeros((tokens, extra), jnp.bfloat16)], axis=1)
    sums = tuple([None] * tile_count for _ in range(3))
    for head in range(HEADS):
        first, last, mask = head_window(head)
        scores = dot_nt(queries[:, first:last], own(mask, key_rows[:, first:last]))
        probs = softmax(scores * scaling + bias_space[head])
        back_one(head, queries, key_rows, values, probs, dc_space, sums)
    stack_grads(*sums)
    grad_normed = dot_nn(stacked[...], proj_space_t[...]).astype(jnp.bfloat16)
    weighted = grad_normed.astype(jnp.float32) * gain_row(gain_space_ref)
    cubed = inv_space * inv_space * inv_space
    mean_wh = jnp.mean(weighted * after[...], axis=-1, keepdims=True)
    grad_after = cot_ref[...].astype(jnp.float32) + (
        inv_space * weighted - after[...] * cubed * mean_wh
    )
    after[...] = grad_after

    rounded = grad_after.astype(jnp.bfloat16)
    dc_moves = [
        exchange(chunk_count + 2, send_dc, got_dc, 0, cut),
        exchange(chunk_count + 3, send_dc, got_dc, cut, wide),
    ]
    send_dc[:, :, :cut] = split(dot_nn(rounded, out_time_t[:, :cut]))
    dc_moves[0][0]()
    grad_ctx = dot_nn(rounded, out_time_t[:, cut:])
    lane = lax.broadcasted_iota(jnp.int32, (1, wide - cut), 1) + cut
    high = inv_time.astype(jnp.bfloat16).astype(jnp.float32)
    spare = jnp.where(lane < HEADS * HD + extra // 2, high, inv_time - high)
    send_dc[:, :, cut:] = split(jnp.where(lane < HEADS * HD, grad_ctx, spare))
    dc_moves[1][0]()
    after_send[...] = after[pl.ds(pl.multiple_of(other * half, half), half), :].astype(jnp.bfloat16)

    def pair_copy(place, source, target):
        return pltpu.make_async_remote_copy(
            src_ref=source,
            dst_ref=target,
            send_sem=pair_send_sems.at[place],
            recv_sem=pair_recv_sems.at[place],
            device_id=(me, other),
            device_id_type=pl.DeviceIdType.MESH,
        )

    after_copy = pair_copy(0, after_send, after_got)
    after_copy.start()

    dc_moves[0][1]()
    dc_time[:, :cut] = merged(got_dc, 0, cut).astype(jnp.bfloat16)
    sums = tuple([None] * tile_count for _ in range(3))
    for head in range(HEADS):
        if head == cut // HD:
            dc_moves[1][1]()
            rest = merged(got_dc, cut, wide)
            place = HEADS * HD - cut
            inv_rows = rest[:, place : place + 1] + rest[:, wide - cut - 1 :]
            dc_time[:, cut:] = rest.astype(jnp.bfloat16)
        back_one(head, q_time, k_time, v_time, probs_time[head], dc_time, sums)
    stack_grads(*sums)
    grad_normed = dot_nn(stacked[...], proj_time_t[...]).astype(jnp.bfloat16).astype(jnp.float32)
    normed = merged(got_normed)
    gain = gain_row(gain_time_ref)
    mean_dn = jnp.mean(grad_normed * normed, axis=-1, keepdims=True)
    total = inv_rows * (
        grad_normed * gain - normed * (1.0 / gain) * mean_dn
    )
    totals[...] = total.reshape(seq_count, rows, width)

    pair_send[...] = totals[pl.ds(other * half_blocks, half_blocks)].astype(jnp.bfloat16)
    total_copy = pair_copy(1, pair_send, pair_got)
    total_copy.start()
    total_copy.wait_recv()
    send_back[...] = (
        totals[pl.ds(core * half_blocks, half_blocks)] + pair_got[...].astype(jnp.float32)
    ).astype(jnp.bfloat16)
    my_slot = lax.rem(me, half_blocks)
    my_half = me // half_blocks

    def back_message(slot):
        return pltpu.make_async_remote_copy(
            src_ref=send_back.at[slot],
            dst_ref=got_back.at[my_slot],
            send_sem=back_send_sems.at[slot],
            recv_sem=back_recv_sems.at[my_slot],
            device_id=(core * half_blocks + slot, my_half),
            device_id_type=pl.DeviceIdType.MESH,
        )

    for slot in range(half_blocks):

        @pl.when(core * half_blocks + slot != me)
        def _(slot=slot):
            back_message(slot).start()

        @pl.when(core * half_blocks + slot == me)
        def _(slot=slot):
            got_back[slot] = send_back[slot]

    after_copy.wait_recv()
    for slot in range(half_blocks):

        @pl.when(core * half_blocks + slot != me)
        def _(slot=slot):
            pltpu.make_async_remote_copy(
                src_ref=send_back.at[slot],
                dst_ref=got_back.at[slot],
                send_sem=back_send_sems.at[slot],
                recv_sem=back_recv_sems.at[slot],
                device_id=(core * half_blocks + slot, my_half),
                device_id_type=pl.DeviceIdType.MESH,
            ).wait_recv()

    out_ref[...] = (
        after[pl.ds(pl.multiple_of(core * half, half), half), :]
        + after_got[...].astype(jnp.float32)
        + got_back[...].astype(jnp.float32).reshape(half, width)
    )
    for slot in range(half_blocks):

        @pl.when(core * half_blocks + slot != me)
        def _(slot=slot):
            back_message(slot).wait_send()

    for _, _, finish in (*normed_moves, *ctx_moves, *dc_moves):
        finish()
    for copy in (*pair_copies, after_copy, total_copy):
        copy.wait_send()


def fused_device(
    clip,
    offsets,
    cotangent,
    gain_time,
    gain_space,
    proj_time,
    out_time,
    proj_space,
    out_space,
    bias_time,
    bias_space,
):
    seq_count = lax.axis_size("seq")
    tokens, width = clip.shape[1:]
    rows = tokens // seq_count
    head_cols = HEADS * HD
    wide = -(-head_cols // LANES) * LANES
    half, half_blocks = tokens // 2, seq_count // 2
    moves = -(-width // (4 * LANES)) + 4
    f32, bf16 = jnp.float32, jnp.bfloat16
    vmem = pltpu.VMEM
    dma = pltpu.SemaphoreType.DMA
    scratch = [
        vmem((tokens, width), bf16),
        vmem((tokens, width), bf16),
        vmem((tokens, width), bf16),
        vmem((width // LANES, LANES), f32),
        vmem((width // LANES, LANES), f32),
        vmem((HEADS * seq_count, seq_count), f32),
        vmem((3 * head_cols, width), bf16),
        vmem((width, wide), bf16),
        vmem((3 * head_cols, width), bf16),
        vmem((width, 3 * head_cols), bf16),
        vmem((wide, width), bf16),
        vmem((width, 3 * head_cols), bf16),
        vmem((wide, width), bf16),
        vmem((HEADS, tokens, tokens), f32),
        vmem((HEADS, tokens, tokens), f32),
        vmem((tokens, width), f32),
        vmem((tokens, width), f32),
        vmem((tokens, wide), bf16),
        vmem((tokens, wide), bf16),
        vmem((tokens, wide), bf16),
        vmem((HEADS, tokens, tokens), f32),
        vmem((tokens, 3 * head_cols), bf16),
        vmem((tokens, wide), bf16),
        vmem((tokens, wide), bf16),
        vmem((seq_count, rows, width), bf16),
        vmem((seq_count, rows, width), bf16),
        vmem((seq_count, rows, wide), bf16),
        vmem((seq_count, rows, wide), bf16),
        vmem((seq_count, rows, wide), bf16),
        vmem((seq_count, rows, wide), bf16),
        vmem((seq_count, rows, width), f32),
        vmem((half_blocks, rows, width), bf16),
        vmem((half_blocks, rows, width), bf16),
        vmem((half_blocks, rows, width), bf16),
        vmem((half_blocks, rows, width), bf16),
        vmem((half, width), bf16),
        vmem((half, width), bf16),
        dma((moves, seq_count)),
        dma((moves, seq_count)),
        dma((half_blocks,)),
        dma((half_blocks,)),
        dma((5,)),
        dma((5,)),
        dma((5,)),
        dma((2,)),
        dma((2,)),
        dma((6,)),
    ]
    out_vmem = pl.BlockSpec(memory_space=pltpu.VMEM)
    anywhere = pl.BlockSpec(memory_space=pl.ANY)
    out = pl.pallas_call(
        functools.partial(fused_kernel, seq_count),
        out_shape=jax.ShapeDtypeStruct((half, width), f32),
        in_specs=[anywhere] * 11,
        out_specs=out_vmem,
        scratch_shapes=scratch,
        compiler_params=pltpu.CompilerParams(
            collective_id=0, has_side_effects=True, vmem_limit_bytes=56 * 1024 * 1024
        ),
    )(
        clip[0],
        offsets[0, 0],
        cotangent[0, 0],
        gain_time.reshape(-1, LANES),
        gain_space.reshape(-1, LANES),
        bias_time.reshape(HEADS * bias_time.shape[1], bias_time.shape[2]),
        proj_time,
        out_time,
        proj_space,
        out_space,
        bias_space,
    )
    return out[None]


def on_device(clip, *rest):
    seq_count = lax.axis_size("seq")
    tokens = clip.shape[1]
    fits = (
        lax.axis_size("dp") == 2
        and clip.shape[0] == 1
        and seq_count & (seq_count - 1) == 0
        and tokens == 8 * seq_count
        and tokens == LANES
        and clip.shape[2] % LANES == 0
    )
    return (fused_device if fits else per_device)(clip, *rest)


def solution(mesh):
    in_specs = (
        P("seq", None, None),
        P("dp", "seq", None, None),
        P("dp", "seq", None, None),
        P(),
        P(),
        P("dp", None),
        P("dp", None),
        P("dp", None),
        P("dp", None),
        P(),
        P(None, "dp", None),
    )
    out_specs = P("seq", "dp", None)
    return jax.shard_map(
        on_device, mesh=mesh, in_specs=in_specs, out_specs=out_specs, check_vma=False
    )
```

profile of v0, /device:TPU:1, one launch (start us, length us, event | category | flops | bytes accessed | tf_op | source)
XLA Modules:
  0.0 46.1 jit_solution(4702764675884819296)
XLA Ops:
  0.0 44.4 %shard_map.109 = f32[64,1152]{1,0:T(8,128)} custom-call(bf16[128,1152]{1,0:T(8,128)(2,1)} %bitcast.8, bf16[128,1152]{1,0:T(8,128)(2,1)} %bitcast.9, bf16[128,1152]{1,0:T(8,128)(2,1)} %bitcast.10, f32[9,128]{1,0:T(8,128)} %bitcast.12, f32[9,128]{1,0:T(8,128)} %bitcast.13, f32[128,16]{1,0:T(8,128)} %bitcast.11, bf16[576,1728]{1,0:T(8,128)(2,1)} %proj_time_in.1, ...), custom_call_target="tpu_custom_call" | custom-call | tf_op jit(solution)/shard_map/pallas_call | solution.py:751
  44.4 1.7 %copy.13 = f32[1,64,1152]{2,1,0:T(8,128)} copy(f32[1,64,1152]{2,1,0:T(8,128)} %bitcast.7) | data formatting | bytes 589824
where the time goes:
time: 46.3 us; the launch traced here: 46.1 us
  Pallas kernels  44.4 us (96%)
  local copies, waits for them, and re-layouts  1.69 us (4%)
    pallas_call x1, Pallas kernels, fused_device(): pl.pallas_call(functools.partial(fused_kernel, seq_count), out_shape=jax....  44.4 us
    unnamed x1, local copies, waits for them, and re-layouts  1.69 us

commit v1 on v0

--- a/solution.py
+++ b/solution.py
@@ -210,12 +210,25 @@
     return lax.dot_general(left, right, (((0,), (0,)), ((), ())), preferred_element_type=jnp.float32)
 
 
-def head_window(head):
-    low, high = head * HD, (head + 1) * HD
-    first = low // LANES * LANES
-    last = -(-high // LANES) * LANES
+def pair_window(pair):
+    first = 2 * pair * HD // LANES * LANES
+    last = -(-2 * (pair + 1) * HD // LANES) * LANES
+    return first, last
+
+
+def head_lanes(head, first, last):
     lane = lax.broadcasted_iota(jnp.int32, (1, last - first), 1) + first
-    return first, last, (lane >= low) & (lane < high)
+    return (lane >= head * HD) & (lane < (head + 1) * HD)
+
+
+def two_heads(block, pair):
+    first, last = pair_window(pair)
+    piece = block[:, first:last]
+    rows = [
+        jnp.where(head_lanes(head, first, last), piece, jnp.zeros_like(piece))
+        for head in (2 * pair, 2 * pair + 1)
+    ]
+    return jnp.concatenate(rows, axis=0)
 
 
 def add_tiles(tiles, first, block):
@@ -225,9 +238,37 @@
         tiles[tile] = piece if tiles[tile] is None else tiles[tile] + piece
 
 
-def softmax(scores):
-    exp_scores = jnp.exp(scores - jnp.max(scores, axis=-1, keepdims=True))
-    return exp_scores * (1.0 / jnp.sum(exp_scores, axis=-1, keepdims=True))
+def pick_tiles(blocks, tokens, tile_count):
+    tiles = []
+    for tile in range(tile_count):
+        low, high = tile * LANES, (tile + 1) * LANES
+        value = jnp.zeros((tokens, LANES), jnp.float32)
+        for head in range(HEADS):
+            if head * HD < high and (head + 1) * HD > low:
+                first, _ = pair_window(head // 2)
+                row = head % 2 * tokens
+                piece = blocks[head // 2][row : row + tokens, low - first : high - first]
+                value = jnp.where(head_lanes(head, low, high), piece, value)
+        tiles.append(value)
+    return tiles
+
+
+def softmax_keys(scores, tokens):
+    halves = []
+    for row in range(0, scores.shape[0], tokens):
+        block = scores[row : row + tokens]
+        exp_block = jnp.exp(block - jnp.max(block, axis=0, keepdims=True))
+        halves.append(exp_block * (1.0 / jnp.sum(exp_block, axis=0, keepdims=True)))
+    return jnp.concatenate(halves, axis=0)
+
+
+def score_grads(grad_probs, probs, tokens, scaling):
+    halves = []
+    for row in range(0, probs.shape[0], tokens):
+        weights, grads = probs[row : row + tokens], grad_probs[row : row + tokens]
+        mean = jnp.sum(grads * weights, axis=0, keepdims=True)
+        halves.append((weights * (grads - mean) * scaling).astype(jnp.bfloat16))
+    return jnp.concatenate(halves, axis=0)
 
 
 def fused_kernel(
@@ -258,6 +299,7 @@
     proj_space,
     out_space,
     bias_space,
+    bias_turned,
     bias_wide,
     hidden,
     after,
@@ -283,8 +325,7 @@
     after_got,
     send_sems,
     recv_sems,
-    back_send_sems,
-    back_recv_sems,
+    back_sems,
     weight_sems,
     weight_send_sems,
     weight_recv_sems,
@@ -313,8 +354,8 @@
             barrier, inc=1, device_id=(peer, other), device_id_type=pl.DeviceIdType.MESH
         )
 
-    inputs = (clip_in, off_in, gain_time_in, bias_time_in, cot_in, gain_space_in)
-    places = (clip_ref, off_ref, gain_time_ref, bias_time_ref, cot_ref, gain_space_ref)
+    inputs = (clip_in, off_in, gain_time_in, cot_in, bias_time_in, gain_space_in)
+    places = (clip_ref, off_ref, gain_time_ref, cot_ref, bias_time_ref, gain_space_ref)
     input_copies = [
         pltpu.make_async_copy(source, target, input_sems.at[place])
         for place, (source, target) in enumerate(zip(inputs, places))
@@ -349,7 +390,6 @@
                 device_id_type=pl.DeviceIdType.MESH,
             )
         )
-        own_copies[-1].start()
 
     def weight_ready(place):
         own_copies[place].wait()
@@ -366,29 +406,33 @@
     def exchange(phase, sent, got, first, last):
         columns = pl.ds(first, last - first)
 
-        def message(step, landing):
-            target = partner(step)
+        def start():
+            for step in range(seq_count - 1, -1, -1):
+                target = partner(step)
+                pltpu.make_async_remote_copy(
+                    src_ref=sent.at[target, :, columns],
+                    dst_ref=got.at[me, :, columns],
+                    send_sem=send_sems.at[phase],
+                    recv_sem=recv_sems.at[phase],
+                    device_id=(target, other),
+                    device_id_type=pl.DeviceIdType.MESH,
+                ).start()
+
+        def whole():
             return pltpu.make_async_remote_copy(
-                src_ref=sent.at[target, :, columns],
-                dst_ref=got.at[landing(target), :, columns],
-                send_sem=send_sems.at[phase, step],
-                recv_sem=recv_sems.at[phase, step],
-                device_id=(target, core),
+                src_ref=sent.at[:, :, columns],
+                dst_ref=got.at[:, :, columns],
+                send_sem=send_sems.at[phase],
+                recv_sem=recv_sems.at[phase],
+                device_id=(me, other),
                 device_id_type=pl.DeviceIdType.MESH,
             )
 
-        def start():
-            for step in range(seq_count - 1, 0, -1):
-                message(step, lambda target: me).start()
-            got[me, :, first:last] = sent[me, :, first:last]
-
         def arrive():
-            for step in range(seq_count - 1, 0, -1):
-                message(step, lambda target: target).wait_recv()
+            whole().wait_recv()
 
         def finish():
-            for step in range(1, seq_count):
-                message(step, lambda target: me).wait_send()
+            whole().wait_send()
 
         return start, arrive, finish
 
@@ -434,21 +478,22 @@
         stacked[:, whole + LANES : 2 * head_cols] = dk[:, LANES:].astype(jnp.bfloat16)
         stacked[:, 2 * head_cols :] = dv[:, :head_cols].astype(jnp.bfloat16)
 
-    def own(mask, block):
-        return jnp.where(mask, block, jnp.zeros_like(block))
-
-    def back_one(head, queries, key_rows, values, probs, grad_ctx, sums):
-        first, last, mask = head_window(head)
-        dq, dk, dv = sums
-        query, key, value, dc = (
-            ref[:, first:last] for ref in (queries, key_rows, values, grad_ctx)
-        )
-        add_tiles(dv, first, dot_tn(probs.astype(jnp.bfloat16), own(mask, dc)))
-        dw = dot_nt(dc, own(mask, value))
-        mean_dw = jnp.sum(dw * probs, axis=-1, keepdims=True)
-        ds = (probs * (dw - mean_dw) * scaling).astype(jnp.bfloat16)
-        add_tiles(dq, first, dot_nn(ds, own(mask, key)))
-        add_tiles(dk, first, dot_tn(ds, own(mask, query)))
+    def back(queries, key_rows, grad_ctx, values, probs, pairs):
+        windows = [pair_window(pair) for pair in pairs]
+        ctxs = [grad_ctx[:, first:last] for first, last in windows]
+        grads = [dot_nt(two_heads(values, pair), ctx) for pair, ctx in zip(pairs, ctxs)]
+        dv = [dot_nn(block.astype(jnp.bfloat16), ctx) for block, ctx in zip(probs, ctxs)]
+        ds = [score_grads(grad, block, tokens, scaling) for grad, block in zip(grads, probs)]
+        dk = [dot_nn(block, queries[:, first:last]) for block, (first, last) in zip(ds, windows)]
+        dq = [dot_tn(block, two_heads(key_rows, pair)) for block, pair in zip(ds, pairs)]
+        return dq, dk, dv
+
+    def grads_of(parts):
+        dq, dk, dv = (sum((part[place] for part in parts), []) for place in range(3))
+        tiles = [None] * tile_count
+        for pair, block in enumerate(dq):
+            add_tiles(tiles, pair_window(pair)[0], block)
+        return tiles, pick_tiles(dk, tokens, tile_count), pick_tiles(dv, tokens, tile_count)
 
     def turn(weight, turned):
         for first in range(0, weight.shape[0], LANES):
@@ -456,13 +501,15 @@
 
     tile_count = wide // LANES
 
-    for copy in input_copies:
+    for copy in input_copies[:3]:
         copy.wait()
+    for copy in own_copies:
+        copy.start()
     hidden[...] = clip_ref[...].astype(jnp.float32) + off_ref[...].astype(jnp.float32)
     normed, inv_time = norm(hidden[...], gain_time_ref)
     send_normed[...] = split(normed)
     pl.semaphore_wait(barrier, 2 * seq_count - 1)
-    feature_cuts = [*range(0, width, 4 * LANES), width]
+    feature_cuts = [0, width // (2 * LANES) * LANES + LANES, width]
     chunk_count = len(feature_cuts) - 1
     normed_moves = [
         exchange(place, send_normed, got_normed, feature_cuts[place], feature_cuts[place + 1])
@@ -479,26 +526,29 @@
     frame = lax.broadcasted_iota(jnp.int32, (seq_count, tokens), 0)
     column = lax.broadcasted_iota(jnp.int32, (seq_count, tokens), 1)
     spread = jnp.where(column // rows == frame, 1.0, 0.0).astype(jnp.float32)
-    bias_cols = lax.dot_general(
-        bias_time_ref[...],
-        spread,
-        (((1,), (0,)), ((), ())),
-        precision=lax.Precision.HIGHEST,
-        preferred_element_type=jnp.float32,
-    )
     same = lax.broadcasted_iota(jnp.int32, (tokens, tokens), 0) % rows == (
         lax.broadcasted_iota(jnp.int32, (tokens, tokens), 1) % rows
     )
+    for copy in input_copies[3:]:
+        copy.wait()
     for head in range(HEADS):
-        block = bias_cols[head * seq_count : (head + 1) * seq_count]
+        block = lax.dot_general(
+            bias_time_ref[head * seq_count : (head + 1) * seq_count, :],
+            spread,
+            (((0,), (0,)), ((), ())),
+            precision=lax.Precision.HIGHEST,
+            preferred_element_type=jnp.float32,
+        )
         block = jnp.broadcast_to(block[:, None, :], (seq_count, rows, tokens))
-        bias_wide[head] = jnp.where(same, block.reshape(tokens, tokens), MASKED)
+        row = head % 2 * tokens
+        bias_wide[head // 2, row : row + tokens, :] = jnp.where(
+            same, block.reshape(tokens, tokens), MASKED
+        )
 
     weight_ready(0)
     dc_space[...] = dot_nt(cot_ref[...], out_space[...]).astype(jnp.bfloat16)
 
     weight_ready(1)
-    turn(proj_time, proj_time_t)
 
     def arrived(place):
         normed_moves[place][1]()
@@ -516,18 +566,32 @@
     v_time[:, : HEADS * HD] = values
     ctx = [None] * tile_count
     cut = 2 * LANES
-    heads_first = -(-cut // HD)
     ctx_moves = [
         exchange(chunk_count, send_ctx, got_ctx, 0, cut),
         exchange(chunk_count + 1, send_ctx, got_ctx, cut, wide),
     ]
-    for head in range(HEADS):
-        first, last, mask = head_window(head)
-        scores = dot_nt(q_time[:, first:last], own(mask, k_time[:, first:last]))
-        probs = softmax(scores * scaling + bias_wide[head])
-        probs_time[head] = probs
-        add_tiles(ctx, first, dot_nn(probs.astype(jnp.bfloat16), own(mask, v_time[:, first:last])))
-        if head == heads_first - 1:
+    pair_count = HEADS // 2
+
+    def probabilities(queries, key_rows, bias, pairs):
+        scores = []
+        for pair in pairs:
+            first, last = pair_window(pair)
+            scores.append(dot_nt(two_heads(key_rows, pair), queries[:, first:last]))
+        return [
+            softmax_keys(block * scaling + bias[pair], tokens) for pair, block in zip(pairs, scores)
+        ]
+
+    groups = [range(place, place + 2) for place in range(0, pair_count, 2)]
+    for group in groups:
+        probs = probabilities(q_time, k_time, bias_wide, group)
+        for pair, block in zip(group, probs):
+            probs_time[pair] = block
+            add_tiles(
+                ctx,
+                pair_window(pair)[0],
+                dot_tn(block.astype(jnp.bfloat16), two_heads(v_time, pair)),
+            )
+        if group is groups[0]:
             send_ctx[:, :, :cut] = split(jnp.concatenate(ctx[: cut // LANES], axis=1))
             ctx_moves[0][0]()
     send_ctx[:, :, cut:] = split(jnp.concatenate(ctx[cut // LANES :], axis=1))
@@ -537,6 +601,9 @@
     weight_ready(4)
     turn(proj_space, proj_space_t)
     turn(out_time, out_time_t)
+    for head in range(HEADS):
+        row = head % 2 * tokens
+        bias_turned[head // 2, row : row + tokens, :] = bias_space[head].T
     ctx_moves[0][1]()
     first_part = dot_nn(merged(got_ctx, 0, cut).astype(jnp.bfloat16), out_time[:cut])
     ctx_moves[1][1]()
@@ -548,13 +615,11 @@
         [(0, width, lambda: normed.astype(jnp.bfloat16))], proj_space
     )
     values = jnp.concatenate([values, jnp.zeros((tokens, extra), jnp.bfloat16)], axis=1)
-    sums = tuple([None] * tile_count for _ in range(3))
-    for head in range(HEADS):
-        first, last, mask = head_window(head)
-        scores = dot_nt(queries[:, first:last], own(mask, key_rows[:, first:last]))
-        probs = softmax(scores * scaling + bias_space[head])
-        back_one(head, queries, key_rows, values, probs, dc_space, sums)
-    stack_grads(*sums)
+    parts = []
+    for group in groups:
+        probs = probabilities(queries, key_rows, bias_turned, group)
+        parts.append(back(queries, key_rows, dc_space, values, probs, group))
+    stack_grads(*grads_of(parts))
     grad_normed = dot_nn(stacked[...], proj_space_t[...]).astype(jnp.bfloat16)
     weighted = grad_normed.astype(jnp.float32) * gain_row(gain_space_ref)
     cubed = inv_space * inv_space * inv_space
@@ -592,18 +657,19 @@
     after_copy = pair_copy(0, after_send, after_got)
     after_copy.start()
 
+    turn(proj_time, proj_time_t)
     dc_moves[0][1]()
     dc_time[:, :cut] = merged(got_dc, 0, cut).astype(jnp.bfloat16)
-    sums = tuple([None] * tile_count for _ in range(3))
-    for head in range(HEADS):
-        if head == cut // HD:
-            dc_moves[1][1]()
-            rest = merged(got_dc, cut, wide)
-            place = HEADS * HD - cut
-            inv_rows = rest[:, place : place + 1] + rest[:, wide - cut - 1 :]
-            dc_time[:, cut:] = rest.astype(jnp.bfloat16)
-        back_one(head, q_time, k_time, v_time, probs_time[head], dc_time, sums)
-    stack_grads(*sums)
+    dc_moves[1][1]()
+    rest = merged(got_dc, cut, wide)
+    place = HEADS * HD - cut
+    inv_rows = rest[:, place : place + 1] + rest[:, wide - cut - 1 :]
+    dc_time[:, cut:] = rest.astype(jnp.bfloat16)
+    parts = []
+    for group in groups:
+        probs = [probs_time[pair] for pair in group]
+        parts.append(back(q_time, k_time, dc_time, v_time, probs, group))
+    stack_grads(*grads_of(parts))
     grad_normed = dot_nn(stacked[...], proj_time_t[...]).astype(jnp.bfloat16).astype(jnp.float32)
     normed = merged(got_normed)
     gain = gain_row(gain_time_ref)
@@ -613,61 +679,41 @@
     )
     totals[...] = total.reshape(seq_count, rows, width)
 
-    pair_send[...] = totals[pl.ds(other * half_blocks, half_blocks)].astype(jnp.bfloat16)
+    pair_send[...] = totals[pl.ds(core * half_blocks, half_blocks)].astype(jnp.bfloat16)
     total_copy = pair_copy(1, pair_send, pair_got)
     total_copy.start()
     total_copy.wait_recv()
     send_back[...] = (
-        totals[pl.ds(core * half_blocks, half_blocks)] + pair_got[...].astype(jnp.float32)
+        totals[pl.ds(other * half_blocks, half_blocks)] + pair_got[...].astype(jnp.float32)
     ).astype(jnp.bfloat16)
     my_slot = lax.rem(me, half_blocks)
     my_half = me // half_blocks
 
-    def back_message(slot):
-        return pltpu.make_async_remote_copy(
+    for slot in range(half_blocks):
+        pltpu.make_async_remote_copy(
             src_ref=send_back.at[slot],
             dst_ref=got_back.at[my_slot],
-            send_sem=back_send_sems.at[slot],
-            recv_sem=back_recv_sems.at[my_slot],
-            device_id=(core * half_blocks + slot, my_half),
+            send_sem=back_sems.at[0],
+            recv_sem=back_sems.at[1],
+            device_id=(other * half_blocks + slot, my_half),
             device_id_type=pl.DeviceIdType.MESH,
-        )
-
-    for slot in range(half_blocks):
-
-        @pl.when(core * half_blocks + slot != me)
-        def _(slot=slot):
-            back_message(slot).start()
-
-        @pl.when(core * half_blocks + slot == me)
-        def _(slot=slot):
-            got_back[slot] = send_back[slot]
-
+        ).start()
+    whole_back = pltpu.make_async_remote_copy(
+        src_ref=send_back,
+        dst_ref=got_back,
+        send_sem=back_sems.at[0],
+        recv_sem=back_sems.at[1],
+        device_id=(me, other),
+        device_id_type=pl.DeviceIdType.MESH,
+    )
     after_copy.wait_recv()
-    for slot in range(half_blocks):
-
-        @pl.when(core * half_blocks + slot != me)
-        def _(slot=slot):
-            pltpu.make_async_remote_copy(
-                src_ref=send_back.at[slot],
-                dst_ref=got_back.at[slot],
-                send_sem=back_send_sems.at[slot],
-                recv_sem=back_recv_sems.at[slot],
-                device_id=(core * half_blocks + slot, my_half),
-                device_id_type=pl.DeviceIdType.MESH,
-            ).wait_recv()
-
+    whole_back.wait_recv()
     out_ref[...] = (
         after[pl.ds(pl.multiple_of(core * half, half), half), :]
         + after_got[...].astype(jnp.float32)
         + got_back[...].astype(jnp.float32).reshape(half, width)
     )
-    for slot in range(half_blocks):
-
-        @pl.when(core * half_blocks + slot != me)
-        def _(slot=slot):
-            back_message(slot).wait_send()
-
+    whole_back.wait_send()
     for _, _, finish in (*normed_moves, *ctx_moves, *dc_moves):
         finish()
     for copy in (*pair_copies, after_copy, total_copy):
@@ -693,7 +739,7 @@
     head_cols = HEADS * HD
     wide = -(-head_cols // LANES) * LANES
     half, half_blocks = tokens // 2, seq_count // 2
-    moves = -(-width // (4 * LANES)) + 4
+    moves = 6
     f32, bf16 = jnp.float32, jnp.bfloat16
     vmem = pltpu.VMEM
     dma = pltpu.SemaphoreType.DMA
@@ -712,13 +758,14 @@
         vmem((width, 3 * head_cols), bf16),
         vmem((wide, width), bf16),
         vmem((HEADS, tokens, tokens), f32),
-        vmem((HEADS, tokens, tokens), f32),
+        vmem((HEADS // 2, 2 * tokens, tokens), f32),
+        vmem((HEADS // 2, 2 * tokens, tokens), f32),
         vmem((tokens, width), f32),
         vmem((tokens, width), f32),
         vmem((tokens, wide), bf16),
         vmem((tokens, wide), bf16),
         vmem((tokens, wide), bf16),
-        vmem((HEADS, tokens, tokens), f32),
+        vmem((HEADS // 2, 2 * tokens, tokens), f32),
         vmem((tokens, 3 * head_cols), bf16),
         vmem((tokens, wide), bf16),
         vmem((tokens, wide), bf16),
@@ -735,10 +782,9 @@
         vmem((half_blocks, rows, width), bf16),
         vmem((half, width), bf16),
         vmem((half, width), bf16),
-        dma((moves, seq_count)),
-        dma((moves, seq_count)),
-        dma((half_blocks,)),
-        dma((half_blocks,)),
+        dma((moves,)),
+        dma((moves,)),
+        dma((2,)),
         dma((5,)),
         dma((5,)),
         dma((5,)),
@@ -750,7 +796,7 @@
     anywhere = pl.BlockSpec(memory_space=pl.ANY)
     out = pl.pallas_call(
         functools.partial(fused_kernel, seq_count),
-        out_shape=jax.ShapeDtypeStruct((half, width), f32),
+        out_shape=pltpu.VMEM((half, width), f32),
         in_specs=[anywhere] * 11,
         out_specs=out_vmem,
         scratch_shapes=scratch,

time: 46.3 us -> 38.5 us (0.83)
  Pallas kernels: 44.4 us -> 37.6 us
  local copies, waits for them, and re-layouts: 1.69 us -> 0.72 us
    pallas_call x1, Pallas kernels: 44.4 us -> 37.6 us  [fused_device(): pl.pallas_call(functools.partial(fused_kernel, seq_count), out_shape=pltp...]
    unnamed x1, local copies, waits for them, and re-layouts: 1.69 us -> 0.72 us
where the time goes in v1:
time: 38.5 us; the launch traced here: 38.4 us
  Pallas kernels  37.6 us (98%)
  local copies, waits for them, and re-layouts  0.72 us (2%)
    pallas_call x1, Pallas kernels, fused_device(): pl.pallas_call(functools.partial(fused_kernel, seq_count), out_shape=pltp...  37.6 us

profile of v1, /device:TPU:1, one launch (start us, length us, event | category | flops | bytes accessed | tf_op | source)
XLA Modules:
  0.0 38.4 jit_solution(11032233667649508470)
XLA Ops:
  0.0 37.6 %shard_map.109 = f32[64,1152]{1,0:T(8,128)S(1)} custom-call(bf16[128,1152]{1,0:T(8,128)(2,1)} %bitcast.8, bf16[128,1152]{1,0:T(8,128)(2,1)} %bitcast.9, bf16[128,1152]{1,0:T(8,128)(2,1)} %bitcast.10, f32[9,128]{1,0:T(8,128)} %bitcast.12, f32[9,128]{1,0:T(8,128)} %bitcast.13, f32[128,16]{1,0:T(8,128)} %bitcast.11, bf16[576,1728]{1,0:T(8,128)(2,1)} %proj_time_in.1, ...), custom_call_target="tpu_custom_call" | custom-call | tf_op jit(solution)/shard_map/pallas_call | solution.py:797
  37.6 0.7 %copy.13 = f32[1,64,1152]{2,1,0:T(8,128)} copy(f32[1,64,1152]{2,1,0:T(8,128)S(1)} %bitcast.7) | data formatting | bytes 589824

commit v2 on v1

--- a/solution.py
+++ b/solution.py
@@ -301,6 +301,10 @@
     bias_space,
     bias_turned,
     bias_wide,
+    fold_in,
+    fold,
+    fold_t,
+    base,
     hidden,
     after,
     q_time,
@@ -452,24 +456,32 @@
         inv_rms = lax.rsqrt(jnp.mean(value * value, axis=-1, keepdims=True) + epsilon)
         return value * inv_rms * gain_row(gain_ref), inv_rms
 
-    def project(chunks, weight):
-        head_cols = HEADS * HD
-        whole = head_cols // LANES * LANES
-        cuts = ((0, whole), (whole, 2 * head_cols), (2 * head_cols, 3 * head_cols))
-        sums = None
-        for first, last, give in chunks:
-            block = give()
-            terms = [dot_nn(block, weight[first:last, low:high]) for low, high in cuts]
-            sums = terms if sums is None else [a + b for a, b in zip(sums, terms)]
+    head_cols = HEADS * HD
+    whole_cols = head_cols // LANES * LANES
+    cuts = ((0, whole_cols), (whole_cols, 2 * head_cols), (2 * head_cols, 3 * head_cols))
+
+    def project(block, weight):
+        return [dot_nn(block, weight[:, low:high]) for low, high in cuts]
+
+    def add(sums, terms):
+        return [a + b for a, b in zip(sums, terms)]
+
+    def by_heads(sums):
         left, middle, values = sums
         queries = jnp.concatenate([left, middle[:, :LANES]], axis=1)
-        key_rows = pltpu.roll(middle, middle.shape[1] - (head_cols - whole), 1)
+        key_rows = pltpu.roll(middle, middle.shape[1] - (head_cols - whole_cols), 1)
         return queries.astype(jnp.bfloat16), key_rows.astype(jnp.bfloat16), values.astype(jnp.bfloat16)
 
+    def weighted_sum(grads, stacks):
+        total = None
+        for tiles, stack in zip(grads, stacks):
+            for tile, value in enumerate(tiles):
+                term = value * stack[:, tile * LANES : (tile + 1) * LANES].astype(jnp.float32)
+                total = term if total is None else total + term
+        return jnp.sum(total, axis=-1, keepdims=True)
+
     def stack_grads(dq, dk, dv):
-        head_cols = HEADS * HD
-        whole = head_cols // LANES * LANES
-        count = len(dq)
+        whole = whole_cols
         dq = jnp.concatenate(dq, axis=1)
         dk = pltpu.roll(jnp.concatenate(dk, axis=1), head_cols - whole, 1)
         dv = jnp.concatenate(dv, axis=1)
@@ -554,16 +566,15 @@
         normed_moves[place][1]()
         return merged(got_normed, feature_cuts[place], feature_cuts[place + 1]).astype(jnp.bfloat16)
 
-    queries, key_rows, values = project(
-        [
-            (feature_cuts[place], feature_cuts[place + 1], functools.partial(arrived, place))
-            for place in range(chunk_count)
-        ],
-        proj_time,
-    )
+    sums = project(arrived(0), proj_time.at[: feature_cuts[1]])
+    for place in range(1, chunk_count):
+        rows_of = proj_time.at[feature_cuts[place] : feature_cuts[place + 1]]
+        sums = add(sums, project(arrived(place), rows_of))
+    queries, key_rows, values = by_heads(sums)
     q_time[...] = queries
     k_time[...] = key_rows
     v_time[:, : HEADS * HD] = values
+    v_time[:, HEADS * HD :] = jnp.zeros((tokens, extra), jnp.bfloat16)
     ctx = [None] * tile_count
     cut = 2 * LANES
     ctx_moves = [
@@ -582,6 +593,7 @@
         ]
 
     groups = [range(place, place + 2) for place in range(0, pair_count, 2)]
+    whole_group = [range(pair_count)]
     for group in groups:
         probs = probabilities(q_time, k_time, bias_wide, group)
         for pair, block in zip(group, probs):
@@ -599,49 +611,60 @@
     weight_ready(2)
     weight_ready(3)
     weight_ready(4)
-    turn(proj_space, proj_space_t)
+    gain = gain_row(gain_space_ref)
+    fold_in[:wide, :] = (out_time[...].astype(jnp.float32) * gain).astype(jnp.bfloat16)
+    fold_in[wide:, :] = (hidden[...] * gain).astype(jnp.bfloat16)
+    for low, high in cuts:
+        block = dot_nn(fold_in[...], proj_space[:, low:high])
+        fold[:, low:high] = block[:wide].astype(jnp.bfloat16)
+        base[:, low:high] = block[wide:]
+    turn(fold, fold_t)
     turn(out_time, out_time_t)
+    cot_ctx = dot_nn(cot_ref[...], out_time_t[...])
     for head in range(HEADS):
         row = head % 2 * tokens
         bias_turned[head // 2, row : row + tokens, :] = bias_space[head].T
     ctx_moves[0][1]()
-    first_part = dot_nn(merged(got_ctx, 0, cut).astype(jnp.bfloat16), out_time[:cut])
+    block = merged(got_ctx, 0, cut).astype(jnp.bfloat16)
+    first_part = hidden[...] + dot_nn(block, out_time[:cut])
+    sums = add([base[:, low:high] for low, high in cuts], project(block, fold.at[:cut]))
     ctx_moves[1][1]()
-
-    second_part = dot_nn(merged(got_ctx, cut, wide).astype(jnp.bfloat16), out_time[cut:])
-    after[...] = hidden[...] + (first_part + second_part)
-    normed, inv_space = norm(after[...], gain_space_ref)
-    queries, key_rows, values = project(
-        [(0, width, lambda: normed.astype(jnp.bfloat16))], proj_space
-    )
+    block = merged(got_ctx, cut, wide).astype(jnp.bfloat16)
+    after_value = first_part + dot_nn(block, out_time[cut:])
+    after[...] = after_value
+    inv_space = lax.rsqrt(jnp.mean(after_value * after_value, axis=-1, keepdims=True) + epsilon)
+    sums = add(sums, project(block, fold.at[cut:]))
+    queries, key_rows, values = by_heads([inv_space * part for part in sums])
     values = jnp.concatenate([values, jnp.zeros((tokens, extra), jnp.bfloat16)], axis=1)
     parts = []
-    for group in groups:
+    for group in whole_group:
         probs = probabilities(queries, key_rows, bias_turned, group)
         parts.append(back(queries, key_rows, dc_space, values, probs, group))
-    stack_grads(*grads_of(parts))
-    grad_normed = dot_nn(stacked[...], proj_space_t[...]).astype(jnp.bfloat16)
-    weighted = grad_normed.astype(jnp.float32) * gain_row(gain_space_ref)
-    cubed = inv_space * inv_space * inv_space
-    mean_wh = jnp.mean(weighted * after[...], axis=-1, keepdims=True)
-    grad_after = cot_ref[...].astype(jnp.float32) + (
-        inv_space * weighted - after[...] * cubed * mean_wh
-    )
-    after[...] = grad_after
-
-    rounded = grad_after.astype(jnp.bfloat16)
+    after_ctx = dot_nn(after[...].astype(jnp.bfloat16), out_time_t[...])
+    grads = grads_of(parts)
+    stack_grads(*grads)
+    lean = weighted_sum(grads, (queries, key_rows, values)) * (inv_space * inv_space / width)
+    rest_ctx = cot_ctx - lean * after_ctx
     dc_moves = [
         exchange(chunk_count + 2, send_dc, got_dc, 0, cut),
         exchange(chunk_count + 3, send_dc, got_dc, cut, wide),
     ]
-    send_dc[:, :, :cut] = split(dot_nn(rounded, out_time_t[:, :cut]))
+    send_dc[:, :, :cut] = split(
+        rest_ctx[:, :cut] + inv_space * dot_nn(stacked[...], fold_t[:, :cut])
+    )
     dc_moves[0][0]()
-    grad_ctx = dot_nn(rounded, out_time_t[:, cut:])
+    grad_ctx = rest_ctx[:, cut:] + inv_space * dot_nn(stacked[...], fold_t[:, cut:])
     lane = lax.broadcasted_iota(jnp.int32, (1, wide - cut), 1) + cut
     high = inv_time.astype(jnp.bfloat16).astype(jnp.float32)
     spare = jnp.where(lane < HEADS * HD + extra // 2, high, inv_time - high)
     send_dc[:, :, cut:] = split(jnp.where(lane < HEADS * HD, grad_ctx, spare))
     dc_moves[1][0]()
+    turn(proj_space, proj_space_t)
+    grad_normed = dot_nn(stacked[...], proj_space_t[...])
+    grad_after = (
+        cot_ref[...].astype(jnp.float32) + inv_space * (grad_normed * gain) - lean * after[...]
+    )
+    after[...] = grad_after
     after_send[...] = after[pl.ds(pl.multiple_of(other * half, half), half), :].astype(jnp.bfloat16)
 
     def pair_copy(place, source, target):
@@ -666,57 +689,75 @@
     inv_rows = rest[:, place : place + 1] + rest[:, wide - cut - 1 :]
     dc_time[:, cut:] = rest.astype(jnp.bfloat16)
     parts = []
-    for group in groups:
+    for group in whole_group:
         probs = [probs_time[pair] for pair in group]
         parts.append(back(q_time, k_time, dc_time, v_time, probs, group))
-    stack_grads(*grads_of(parts))
-    grad_normed = dot_nn(stacked[...], proj_time_t[...]).astype(jnp.bfloat16).astype(jnp.float32)
-    normed = merged(got_normed)
+    grads = grads_of(parts)
+    stack_grads(*grads)
+    lean = weighted_sum(grads, (q_time, k_time, v_time)) * (1.0 / width)
     gain = gain_row(gain_time_ref)
-    mean_dn = jnp.mean(grad_normed * normed, axis=-1, keepdims=True)
-    total = inv_rows * (
-        grad_normed * gain - normed * (1.0 / gain) * mean_dn
-    )
-    totals[...] = total.reshape(seq_count, rows, width)
-
-    pair_send[...] = totals[pl.ds(core * half_blocks, half_blocks)].astype(jnp.bfloat16)
-    total_copy = pair_copy(1, pair_send, pair_got)
-    total_copy.start()
-    total_copy.wait_recv()
-    send_back[...] = (
-        totals[pl.ds(other * half_blocks, half_blocks)] + pair_got[...].astype(jnp.float32)
-    ).astype(jnp.bfloat16)
+    inverse = 1.0 / gain
+    total_copies = []
+    for place in range(chunk_count):
+        low, high = feature_cuts[place], feature_cuts[place + 1]
+        columns = pl.ds(low, high - low)
+        grad_normed = dot_nn(stacked[...], proj_time_t[:, low:high])
+        tilt = merged(got_normed, low, high) * inverse[:, low:high] * lean
+        total = inv_rows * (grad_normed * gain[:, low:high] - tilt)
+        totals[:, :, low:high] = total.reshape(seq_count, rows, high - low)
+        mine = totals.at[pl.ds(core * half_blocks, half_blocks)]
+        pair_send[:, :, low:high] = mine[:, :, low:high].astype(jnp.bfloat16)
+        total_copies.append(
+            pair_copy(1 + place, pair_send.at[:, :, columns], pair_got.at[:, :, columns])
+        )
+        total_copies[-1].start()
     my_slot = lax.rem(me, half_blocks)
     my_half = me // half_blocks
 
-    for slot in range(half_blocks):
-        pltpu.make_async_remote_copy(
-            src_ref=send_back.at[slot],
-            dst_ref=got_back.at[my_slot],
-            send_sem=back_sems.at[0],
-            recv_sem=back_sems.at[1],
-            device_id=(other * half_blocks + slot, my_half),
+    def back_copy(place, slot, source, target, to):
+        return pltpu.make_async_remote_copy(
+            src_ref=source,
+            dst_ref=target,
+            send_sem=back_sems.at[0, place],
+            recv_sem=back_sems.at[1, place],
+            device_id=to,
             device_id_type=pl.DeviceIdType.MESH,
-        ).start()
-    whole_back = pltpu.make_async_remote_copy(
-        src_ref=send_back,
-        dst_ref=got_back,
-        send_sem=back_sems.at[0],
-        recv_sem=back_sems.at[1],
-        device_id=(me, other),
-        device_id_type=pl.DeviceIdType.MESH,
-    )
+        )
+
+    whole_backs = []
+    for place in range(chunk_count):
+        low, high = feature_cuts[place], feature_cuts[place + 1]
+        columns = pl.ds(low, high - low)
+        total_copies[place].wait_recv()
+        kept = totals.at[pl.ds(other * half_blocks, half_blocks)]
+        send_back[:, :, low:high] = (
+            kept[:, :, low:high] + pair_got[:, :, low:high].astype(jnp.float32)
+        ).astype(jnp.bfloat16)
+        for slot in range(half_blocks):
+            back_copy(
+                place,
+                slot,
+                send_back.at[slot, :, columns],
+                got_back.at[my_slot, :, columns],
+                (other * half_blocks + slot, my_half),
+            ).start()
+        whole_backs.append(
+            back_copy(place, 0, send_back.at[:, :, columns], got_back.at[:, :, columns], (me, other))
+        )
     after_copy.wait_recv()
-    whole_back.wait_recv()
-    out_ref[...] = (
-        after[pl.ds(pl.multiple_of(core * half, half), half), :]
-        + after_got[...].astype(jnp.float32)
-        + got_back[...].astype(jnp.float32).reshape(half, width)
-    )
-    whole_back.wait_send()
+    for place in range(chunk_count):
+        low, high = feature_cuts[place], feature_cuts[place + 1]
+        whole_backs[place].wait_recv()
+        out_ref[:, low:high] = (
+            after[pl.ds(pl.multiple_of(core * half, half), half), low:high]
+            + after_got[:, low:high].astype(jnp.float32)
+            + got_back[:, :, low:high].astype(jnp.float32).reshape(half, high - low)
+        )
+    for copy in whole_backs:
+        copy.wait_send()
     for _, _, finish in (*normed_moves, *ctx_moves, *dc_moves):
         finish()
-    for copy in (*pair_copies, after_copy, total_copy):
+    for copy in (*pair_copies, after_copy, *total_copies):
         copy.wait_send()
 
 
@@ -760,6 +801,10 @@
         vmem((HEADS, tokens, tokens), f32),
         vmem((HEADS // 2, 2 * tokens, tokens), f32),
         vmem((HEADS // 2, 2 * tokens, tokens), f32),
+        vmem((wide + tokens, width), bf16),
+        vmem((wide, 3 * head_cols), bf16),
+        vmem((3 * head_cols, wide), bf16),
+        vmem((tokens, 3 * head_cols), f32),
         vmem((tokens, width), f32),
         vmem((tokens, width), f32),
         vmem((tokens, wide), bf16),
@@ -784,12 +829,12 @@
         vmem((half, width), bf16),
         dma((moves,)),
         dma((moves,)),
-        dma((2,)),
+        dma((2, 2)),
         dma((5,)),
         dma((5,)),
         dma((5,)),
-        dma((2,)),
-        dma((2,)),
+        dma((3,)),
+        dma((3,)),
         dma((6,)),
     ]
     out_vmem = pl.BlockSpec(memory_space=pltpu.VMEM)

time: 38.5 us -> 37.3 us (0.969)
  Pallas kernels: 37.6 us -> 36.4 us
    pallas_call x1, Pallas kernels: 37.6 us -> 36.4 us  [fused_device(): pl.pallas_call(functools.partial(fused_kernel, seq_count), out_shape=pltp...]
where the time goes in v2:
time: 37.3 us; the launch traced here: 37.2 us
  Pallas kernels  36.4 us (98%)
  local copies, waits for them, and re-layouts  0.72 us (2%)
    pallas_call x1, Pallas kernels, fused_device(): pl.pallas_call(functools.partial(fused_kernel, seq_count), out_shape=pltp...  36.4 us

profile of v2, /device:TPU:1, one launch (start us, length us, event | category | flops | bytes accessed | tf_op | source)
XLA Modules:
  0.0 37.2 jit_solution(14609571746882732989)
XLA Ops:
  0.0 36.4 %shard_map.109 = f32[64,1152]{1,0:T(8,128)S(1)} custom-call(bf16[128,1152]{1,0:T(8,128)(2,1)} %bitcast.8, bf16[128,1152]{1,0:T(8,128)(2,1)} %bitcast.9, bf16[128,1152]{1,0:T(8,128)(2,1)} %bitcast.10, f32[9,128]{1,0:T(8,128)} %bitcast.12, f32[9,128]{1,0:T(8,128)} %bitcast.13, f32[128,16]{1,0:T(8,128)} %bitcast.11, bf16[576,1728]{1,0:T(8,128)(2,1)} %proj_time_in.1, ...), custom_call_target="tpu_custom_call" | custom-call | tf_op jit(solution)/shard_map/pallas_call | solution.py:842
  36.4 0.7 %copy.13 = f32[1,64,1152]{2,1,0:T(8,128)} copy(f32[1,64,1152]{2,1,0:T(8,128)S(1)} %bitcast.7) | data formatting | bytes 589824

commit v3 on v2

--- a/solution.py
+++ b/solution.py
@@ -320,9 +320,7 @@
     got_ctx,
     send_dc,
     got_dc,
-    totals,
-    pair_send,
-    pair_got,
+    spare_rows,
     send_back,
     got_back,
     after_send,
@@ -344,6 +342,7 @@
     rows = tokens // seq_count
     half = tokens // 2
     half_blocks = seq_count // 2
+    phases = spare_rows.shape[0] - 1
     wide = q_time.shape[1]
     scaling = 1.0 / math.sqrt(HD)
 
@@ -407,20 +406,32 @@
             bit *= 2
         return place
 
+    share_rows = rows // 2
+
+    def share(to):
+        return pl.ds(pl.multiple_of(to * share_rows, share_rows), share_rows)
+
+    def stay(source, target, send_sem, recv_sem, phase):
+        pltpu.make_async_copy(source, target, recv_sem).start()
+        unused = spare_rows.at[phase, pl.ds(0, share_rows), pl.ds(0, source.shape[-1])]
+        pltpu.make_async_copy(source, unused, send_sem).start()
+
     def exchange(phase, sent, got, first, last):
         columns = pl.ds(first, last - first)
 
         def start():
-            for step in range(seq_count - 1, -1, -1):
-                target = partner(step)
+            for step, cross in [(11, 1), (10, 1), (9, 1), (8, 1), (15, 1), (14, 1), (13, 1), (12, 1), (7, 1), (6, 1), (5, 1), (4, 1), (3, 1), (2, 1), (1, 1), (0, 1), (11, 0), (10, 0), (9, 0), (8, 0), (15, 0), (14, 0), (13, 0), (12, 0), (7, 0), (6, 0), (5, 0), (4, 0), (3, 0), (2, 0), (1, 0)]:
+                target, to = partner(step), other if cross else core
                 pltpu.make_async_remote_copy(
-                    src_ref=sent.at[target, :, columns],
-                    dst_ref=got.at[me, :, columns],
+                    src_ref=sent.at[target, share(to), columns],
+                    dst_ref=got.at[me, share(core), columns],
                     send_sem=send_sems.at[phase],
                     recv_sem=recv_sems.at[phase],
-                    device_id=(target, other),
+                    device_id=(target, to),
                     device_id_type=pl.DeviceIdType.MESH,
                 ).start()
+            own = sent.at[me, share(core), columns]
+            stay(own, got.at[me, share(core), columns], send_sems.at[phase], recv_sems.at[phase], phase)
 
         def whole():
             return pltpu.make_async_remote_copy(
@@ -515,13 +526,13 @@
 
     for copy in input_copies[:3]:
         copy.wait()
-    for copy in own_copies:
-        copy.start()
+    for place in (0, 4, 1, 2, 3):
+        own_copies[place].start()
     hidden[...] = clip_ref[...].astype(jnp.float32) + off_ref[...].astype(jnp.float32)
     normed, inv_time = norm(hidden[...], gain_time_ref)
     send_normed[...] = split(normed)
     pl.semaphore_wait(barrier, 2 * seq_count - 1)
-    feature_cuts = [0, width // (2 * LANES) * LANES + LANES, width]
+    feature_cuts = [0, width]
     chunk_count = len(feature_cuts) - 1
     normed_moves = [
         exchange(place, send_normed, got_normed, feature_cuts[place], feature_cuts[place + 1])
@@ -529,8 +540,8 @@
     ]
     for start, _, _ in normed_moves:
         start()
-    for copy in pair_copies:
-        copy.start()
+    for place in (0, 4, 1, 2, 3):
+        pair_copies[place].start()
 
     extra = wide - HEADS * HD
     for ref in (out_time, out_space):
@@ -560,7 +571,17 @@
     weight_ready(0)
     dc_space[...] = dot_nt(cot_ref[...], out_space[...]).astype(jnp.bfloat16)
 
+    weight_ready(4)
+    for head in range(HEADS):
+        row = head % 2 * tokens
+        bias_turned[head // 2, row : row + tokens, :] = bias_space[head].T
     weight_ready(1)
+    weight_ready(2)
+    gain = gain_row(gain_space_ref)
+    fold_in[:wide, :] = (out_time[...].astype(jnp.float32) * gain).astype(jnp.bfloat16)
+    fold_in[wide:, :] = (hidden[...] * gain).astype(jnp.bfloat16)
+    turn(out_time, out_time_t)
+    cot_ctx = dot_nn(cot_ref[...], out_time_t[...])
 
     def arrived(place):
         normed_moves[place][1]()
@@ -577,10 +598,7 @@
     v_time[:, HEADS * HD :] = jnp.zeros((tokens, extra), jnp.bfloat16)
     ctx = [None] * tile_count
     cut = 2 * LANES
-    ctx_moves = [
-        exchange(chunk_count, send_ctx, got_ctx, 0, cut),
-        exchange(chunk_count + 1, send_ctx, got_ctx, cut, wide),
-    ]
+    ctx_move = exchange(chunk_count, send_ctx, got_ctx, 0, wide)
     pair_count = HEADS // 2
 
     def probabilities(queries, key_rows, bias, pairs):
@@ -594,7 +612,7 @@
 
     groups = [range(place, place + 2) for place in range(0, pair_count, 2)]
     whole_group = [range(pair_count)]
-    for group in groups:
+    for group in whole_group:
         probs = probabilities(q_time, k_time, bias_wide, group)
         for pair, block in zip(group, probs):
             probs_time[pair] = block
@@ -603,37 +621,20 @@
                 pair_window(pair)[0],
                 dot_tn(block.astype(jnp.bfloat16), two_heads(v_time, pair)),
             )
-        if group is groups[0]:
-            send_ctx[:, :, :cut] = split(jnp.concatenate(ctx[: cut // LANES], axis=1))
-            ctx_moves[0][0]()
-    send_ctx[:, :, cut:] = split(jnp.concatenate(ctx[cut // LANES :], axis=1))
-    ctx_moves[1][0]()
-    weight_ready(2)
+    send_ctx[...] = split(jnp.concatenate(ctx, axis=1))
+    ctx_move[0]()
     weight_ready(3)
-    weight_ready(4)
-    gain = gain_row(gain_space_ref)
-    fold_in[:wide, :] = (out_time[...].astype(jnp.float32) * gain).astype(jnp.bfloat16)
-    fold_in[wide:, :] = (hidden[...] * gain).astype(jnp.bfloat16)
     for low, high in cuts:
         block = dot_nn(fold_in[...], proj_space[:, low:high])
         fold[:, low:high] = block[:wide].astype(jnp.bfloat16)
         base[:, low:high] = block[wide:]
     turn(fold, fold_t)
-    turn(out_time, out_time_t)
-    cot_ctx = dot_nn(cot_ref[...], out_time_t[...])
-    for head in range(HEADS):
-        row = head % 2 * tokens
-        bias_turned[head // 2, row : row + tokens, :] = bias_space[head].T
-    ctx_moves[0][1]()
-    block = merged(got_ctx, 0, cut).astype(jnp.bfloat16)
-    first_part = hidden[...] + dot_nn(block, out_time[:cut])
-    sums = add([base[:, low:high] for low, high in cuts], project(block, fold.at[:cut]))
-    ctx_moves[1][1]()
-    block = merged(got_ctx, cut, wide).astype(jnp.bfloat16)
-    after_value = first_part + dot_nn(block, out_time[cut:])
+    ctx_move[1]()
+    block = merged(got_ctx).astype(jnp.bfloat16)
+    after_value = hidden[...] + dot_nn(block, out_time[...])
     after[...] = after_value
     inv_space = lax.rsqrt(jnp.mean(after_value * after_value, axis=-1, keepdims=True) + epsilon)
-    sums = add(sums, project(block, fold.at[cut:]))
+    sums = add([base[:, low:high] for low, high in cuts], project(block, fold))
     queries, key_rows, values = by_heads([inv_space * part for part in sums])
     values = jnp.concatenate([values, jnp.zeros((tokens, extra), jnp.bfloat16)], axis=1)
     parts = []
@@ -645,20 +646,13 @@
     stack_grads(*grads)
     lean = weighted_sum(grads, (queries, key_rows, values)) * (inv_space * inv_space / width)
     rest_ctx = cot_ctx - lean * after_ctx
-    dc_moves = [
-        exchange(chunk_count + 2, send_dc, got_dc, 0, cut),
-        exchange(chunk_count + 3, send_dc, got_dc, cut, wide),
-    ]
-    send_dc[:, :, :cut] = split(
-        rest_ctx[:, :cut] + inv_space * dot_nn(stacked[...], fold_t[:, :cut])
-    )
-    dc_moves[0][0]()
-    grad_ctx = rest_ctx[:, cut:] + inv_space * dot_nn(stacked[...], fold_t[:, cut:])
-    lane = lax.broadcasted_iota(jnp.int32, (1, wide - cut), 1) + cut
+    dc_move = exchange(chunk_count + 1, send_dc, got_dc, 0, wide)
+    grad_ctx = rest_ctx + inv_space * dot_nn(stacked[...], fold_t[...])
+    lane = lax.broadcasted_iota(jnp.int32, (1, wide), 1)
     high = inv_time.astype(jnp.bfloat16).astype(jnp.float32)
     spare = jnp.where(lane < HEADS * HD + extra // 2, high, inv_time - high)
-    send_dc[:, :, cut:] = split(jnp.where(lane < HEADS * HD, grad_ctx, spare))
-    dc_moves[1][0]()
+    send_dc[...] = split(jnp.where(lane < HEADS * HD, grad_ctx, spare))
+    dc_move[0]()
     turn(proj_space, proj_space_t)
     grad_normed = dot_nn(stacked[...], proj_space_t[...])
     grad_after = (
@@ -681,13 +675,10 @@
     after_copy.start()
 
     turn(proj_time, proj_time_t)
-    dc_moves[0][1]()
-    dc_time[:, :cut] = merged(got_dc, 0, cut).astype(jnp.bfloat16)
-    dc_moves[1][1]()
-    rest = merged(got_dc, cut, wide)
-    place = HEADS * HD - cut
-    inv_rows = rest[:, place : place + 1] + rest[:, wide - cut - 1 :]
-    dc_time[:, cut:] = rest.astype(jnp.bfloat16)
+    dc_move[1]()
+    block = merged(got_dc)
+    inv_rows = block[:, HEADS * HD : HEADS * HD + 1] + block[:, wide - 1 :]
+    dc_time[...] = block.astype(jnp.bfloat16)
     parts = []
     for group in whole_group:
         probs = [probs_time[pair] for pair in group]
@@ -697,67 +688,55 @@
     lean = weighted_sum(grads, (q_time, k_time, v_time)) * (1.0 / width)
     gain = gain_row(gain_time_ref)
     inverse = 1.0 / gain
-    total_copies = []
-    for place in range(chunk_count):
-        low, high = feature_cuts[place], feature_cuts[place + 1]
-        columns = pl.ds(low, high - low)
-        grad_normed = dot_nn(stacked[...], proj_time_t[:, low:high])
-        tilt = merged(got_normed, low, high) * inverse[:, low:high] * lean
-        total = inv_rows * (grad_normed * gain[:, low:high] - tilt)
-        totals[:, :, low:high] = total.reshape(seq_count, rows, high - low)
-        mine = totals.at[pl.ds(core * half_blocks, half_blocks)]
-        pair_send[:, :, low:high] = mine[:, :, low:high].astype(jnp.bfloat16)
-        total_copies.append(
-            pair_copy(1 + place, pair_send.at[:, :, columns], pair_got.at[:, :, columns])
-        )
-        total_copies[-1].start()
+    tilt = merged(got_normed) * inverse * lean
+    total = inv_rows * (dot_nn(stacked[...], proj_time_t[...]) * gain - tilt)
+    total = total + pltpu.roll(total, tokens - share_rows, 0)
+    send_back[...] = split(total)
     my_slot = lax.rem(me, half_blocks)
     my_half = me // half_blocks
-
-    def back_copy(place, slot, source, target, to):
+    send_sem, recv_sem = back_sems.at[0], back_sems.at[1]
+
+    def back_copy(target):
         return pltpu.make_async_remote_copy(
-            src_ref=source,
-            dst_ref=target,
-            send_sem=back_sems.at[0, place],
-            recv_sem=back_sems.at[1, place],
-            device_id=to,
+            src_ref=send_back.at[target, pl.ds(0, share_rows)],
+            dst_ref=got_back.at[my_slot, share(core)],
+            send_sem=send_sem,
+            recv_sem=recv_sem,
+            device_id=(target, my_half),
             device_id_type=pl.DeviceIdType.MESH,
         )
 
-    whole_backs = []
-    for place in range(chunk_count):
-        low, high = feature_cuts[place], feature_cuts[place + 1]
-        columns = pl.ds(low, high - low)
-        total_copies[place].wait_recv()
-        kept = totals.at[pl.ds(other * half_blocks, half_blocks)]
-        send_back[:, :, low:high] = (
-            kept[:, :, low:high] + pair_got[:, :, low:high].astype(jnp.float32)
-        ).astype(jnp.bfloat16)
-        for slot in range(half_blocks):
-            back_copy(
-                place,
-                slot,
-                send_back.at[slot, :, columns],
-                got_back.at[my_slot, :, columns],
-                (other * half_blocks + slot, my_half),
-            ).start()
-        whole_backs.append(
-            back_copy(place, 0, send_back.at[:, :, columns], got_back.at[:, :, columns], (me, other))
-        )
+    for step in range(seq_count - 1, 0, -1):
+        back_copy(partner(step)).start()
+
+    @pl.when(my_half != core)
+    def _():
+        back_copy(me).start()
+
+    @pl.when(my_half == core)
+    def _():
+        source = send_back.at[me, pl.ds(0, share_rows)]
+        stay(source, got_back.at[my_slot, share(core)], send_sem, recv_sem, phases)
+
+    whole_back = pltpu.make_async_remote_copy(
+        src_ref=send_back.at[pl.ds(0, half_blocks)],
+        dst_ref=got_back,
+        send_sem=send_sem,
+        recv_sem=recv_sem,
+        device_id=(me, other),
+        device_id_type=pl.DeviceIdType.MESH,
+    )
     after_copy.wait_recv()
-    for place in range(chunk_count):
-        low, high = feature_cuts[place], feature_cuts[place + 1]
-        whole_backs[place].wait_recv()
-        out_ref[:, low:high] = (
-            after[pl.ds(pl.multiple_of(core * half, half), half), low:high]
-            + after_got[:, low:high].astype(jnp.float32)
-            + got_back[:, :, low:high].astype(jnp.float32).reshape(half, high - low)
-        )
-    for copy in whole_backs:
-        copy.wait_send()
-    for _, _, finish in (*normed_moves, *ctx_moves, *dc_moves):
+    whole_back.wait_recv()
+    out_ref[...] = (
+        after[pl.ds(pl.multiple_of(core * half, half), half), :]
+        + after_got[...].astype(jnp.float32)
+        + got_back[...].astype(jnp.float32).reshape(half, width)
+    )
+    whole_back.wait_send()
+    for _, _, finish in (*normed_moves, ctx_move, dc_move):
         finish()
-    for copy in (*pair_copies, after_copy, *total_copies):
+    for copy in (*pair_copies, after_copy):
         copy.wait_send()
 
 
@@ -780,7 +759,7 @@
     head_cols = HEADS * HD
     wide = -(-head_cols // LANES) * LANES
     half, half_blocks = tokens // 2, seq_count // 2
-    moves = 6
+    moves = 3
     f32, bf16 = jnp.float32, jnp.bfloat16
     vmem = pltpu.VMEM
     dma = pltpu.SemaphoreType.DMA
@@ -820,21 +799,19 @@
         vmem((seq_count, rows, wide), bf16),
         vmem((seq_count, rows, wide), bf16),
         vmem((seq_count, rows, wide), bf16),
-        vmem((seq_count, rows, width), f32),
-        vmem((half_blocks, rows, width), bf16),
-        vmem((half_blocks, rows, width), bf16),
-        vmem((half_blocks, rows, width), bf16),
+        vmem((moves + 1, rows, width), bf16),
+        vmem((seq_count, rows, width), bf16),
         vmem((half_blocks, rows, width), bf16),
         vmem((half, width), bf16),
         vmem((half, width), bf16),
         dma((moves,)),
         dma((moves,)),
-        dma((2, 2)),
+        dma((2,)),
         dma((5,)),
         dma((5,)),
         dma((5,)),
-        dma((3,)),
-        dma((3,)),
+        dma((1,)),
+        dma((1,)),
         dma((6,)),
     ]
     out_vmem = pl.BlockSpec(memory_space=pltpu.VMEM)

time: 37.3 us -> 36.2 us (0.971)
  Pallas kernels: 36.4 us -> 35.4 us
    pallas_call x1, Pallas kernels: 36.4 us -> 35.4 us  [fused_device(): pl.pallas_call(functools.partial(fused_kernel, seq_count), out_shape=pltp...]
where the time goes in v3:
time: 36.2 us; the launch traced here: 36.1 us
  Pallas kernels  35.4 us (98%)
  local copies, waits for them, and re-layouts  0.72 us (2%)
    pallas_call x1, Pallas kernels, fused_device(): pl.pallas_call(functools.partial(fused_kernel, seq_count), out_shape=pltp...  35.4 us

profile of v3, /device:TPU:1, one launch (start us, length us, event | category | flops | bytes accessed | tf_op | source)
XLA Modules:
  0.0 36.1 jit_solution(18256539034772380226)
XLA Ops:
  0.0 35.4 %shard_map.109 = f32[64,1152]{1,0:T(8,128)S(1)} custom-call(bf16[128,1152]{1,0:T(8,128)(2,1)} %bitcast.8, bf16[128,1152]{1,0:T(8,128)(2,1)} %bitcast.9, bf16[128,1152]{1,0:T(8,128)(2,1)} %bitcast.10, f32[9,128]{1,0:T(8,128)} %bitcast.12, f32[9,128]{1,0:T(8,128)} %bitcast.13, f32[128,16]{1,0:T(8,128)} %bitcast.11, bf16[576,1728]{1,0:T(8,128)(2,1)} %proj_time_in.1, ...), custom_call_target="tpu_custom_call" | custom-call | tf_op jit(solution)/shard_map/pallas_call | solution.py:819
  35.4 0.7 %copy.13 = f32[1,64,1152]{2,1,0:T(8,128)} copy(f32[1,64,1152]{2,1,0:T(8,128)S(1)} %bitcast.7) | data formatting | bytes 589824

commit v4 on v3

--- a/solution.py
+++ b/solution.py
@@ -407,6 +407,9 @@
         return place
 
     share_rows = rows // 2
+    quarter = seq_count // 4
+    far = [*range(3 * quarter - 1, 2 * quarter - 1, -1), *range(seq_count - 1, 3 * quarter - 1, -1)]
+    steps = [*far, *range(2 * quarter - 1, 0, -1)]
 
     def share(to):
         return pl.ds(pl.multiple_of(to * share_rows, share_rows), share_rows)
@@ -420,8 +423,8 @@
         columns = pl.ds(first, last - first)
 
         def start():
-            for step, cross in [(11, 1), (10, 1), (9, 1), (8, 1), (15, 1), (14, 1), (13, 1), (12, 1), (7, 1), (6, 1), (5, 1), (4, 1), (3, 1), (2, 1), (1, 1), (0, 1), (11, 0), (10, 0), (9, 0), (8, 0), (15, 0), (14, 0), (13, 0), (12, 0), (7, 0), (6, 0), (5, 0), (4, 0), (3, 0), (2, 0), (1, 0)]:
-                target, to = partner(step), other if cross else core
+            for step, to in (*[(step, 1) for step in steps], *[(step, 0) for step in steps], (0, other)):
+                target = partner(step)
                 pltpu.make_async_remote_copy(
                     src_ref=sent.at[target, share(to), columns],
                     dst_ref=got.at[me, share(core), columns],
@@ -727,12 +730,10 @@
         device_id_type=pl.DeviceIdType.MESH,
     )
     after_copy.wait_recv()
+    kept = after[pl.ds(pl.multiple_of(core * half, half), half), :]
+    out_ref[...] = kept + after_got[...].astype(jnp.float32)
     whole_back.wait_recv()
-    out_ref[...] = (
-        after[pl.ds(pl.multiple_of(core * half, half), half), :]
-        + after_got[...].astype(jnp.float32)
-        + got_back[...].astype(jnp.float32).reshape(half, width)
-    )
+    out_ref[...] += got_back[...].astype(jnp.float32).reshape(half, width)
     whole_back.wait_send()
     for _, _, finish in (*normed_moves, ctx_move, dc_move):
         finish()

time: 36.2 us -> 35.9 us (level)
  no operation moved by 1% of the time
where the time goes in v4:
time: 35.9 us; the launch traced here: 35.8 us
  Pallas kernels  35.1 us (98%)
  local copies, waits for them, and re-layouts  0.72 us (2%)
    pallas_call x1, Pallas kernels, fused_device(): pl.pallas_call(functools.partial(fused_kernel, seq_count), out_shape=pltp...  35.1 us

profile of v4, /device:TPU:1, one launch (start us, length us, event | category | flops | bytes accessed | tf_op | source)
XLA Modules:
  0.0 35.8 jit_solution(7092989140542600136)
XLA Ops:
  0.0 35.1 %shard_map.109 = f32[64,1152]{1,0:T(8,128)S(1)} custom-call(bf16[128,1152]{1,0:T(8,128)(2,1)} %bitcast.8, bf16[128,1152]{1,0:T(8,128)(2,1)} %bitcast.9, bf16[128,1152]{1,0:T(8,128)(2,1)} %bitcast.10, f32[9,128]{1,0:T(8,128)} %bitcast.12, f32[9,128]{1,0:T(8,128)} %bitcast.13, f32[128,16]{1,0:T(8,128)} %bitcast.11, bf16[576,1728]{1,0:T(8,128)(2,1)} %proj_time_in.1, ...), custom_call_target="tpu_custom_call" | custom-call | tf_op jit(solution)/shard_map/pallas_call | solution.py:820
  35.1 0.7 %copy.13 = f32[1,64,1152]{2,1,0:T(8,128)} copy(f32[1,64,1152]{2,1,0:T(8,128)S(1)} %bitcast.7) | data formatting | bytes 589824

commit v5 on v4

--- a/solution.py
+++ b/solution.py
@@ -321,6 +321,7 @@
     send_dc,
     got_dc,
     spare_rows,
+    spare_ctx,
     send_back,
     got_back,
     after_send,
@@ -330,7 +331,6 @@
     back_sems,
     weight_sems,
     weight_send_sems,
-    weight_recv_sems,
     pair_send_sems,
     pair_recv_sems,
     input_sems,
@@ -388,15 +388,25 @@
                 src_ref=source,
                 dst_ref=target,
                 send_sem=weight_send_sems.at[place],
-                recv_sem=weight_recv_sems.at[place],
+                recv_sem=weight_sems.at[place],
                 device_id=(me, other),
                 device_id_type=pl.DeviceIdType.MESH,
             )
         )
 
     def weight_ready(place):
-        own_copies[place].wait()
-        pair_copies[place].wait_recv()
+        if place == len(sources):
+            full = bias_space
+        else:
+            full = targets[place].at[pl.ds(0, 2 * sources[place].shape[0])]
+        pltpu.make_async_remote_copy(
+            src_ref=full,
+            dst_ref=full,
+            send_sem=weight_send_sems.at[place],
+            recv_sem=weight_sems.at[place],
+            device_id=(me, other),
+            device_id_type=pl.DeviceIdType.MESH,
+        ).wait_recv()
 
     def partner(step):
         place, bit = me, 1
@@ -416,11 +426,14 @@
 
     def stay(source, target, send_sem, recv_sem, phase):
         pltpu.make_async_copy(source, target, recv_sem).start()
-        unused = spare_rows.at[phase, pl.ds(0, share_rows), pl.ds(0, source.shape[-1])]
+        if source.shape[-1] == head_cols:
+            unused = spare_ctx.at[pl.ds(0, share_rows)]
+        else:
+            unused = spare_rows.at[phase, pl.ds(0, share_rows), pl.ds(0, source.shape[-1])]
         pltpu.make_async_copy(source, unused, send_sem).start()
 
     def exchange(phase, sent, got, first, last):
-        columns = pl.ds(first, last - first)
+        columns = slice(None)
 
         def start():
             for step, to in (*[(step, 1) for step in steps], *[(step, 0) for step in steps], (0, other)):
@@ -601,7 +614,7 @@
     v_time[:, HEADS * HD :] = jnp.zeros((tokens, extra), jnp.bfloat16)
     ctx = [None] * tile_count
     cut = 2 * LANES
-    ctx_move = exchange(chunk_count, send_ctx, got_ctx, 0, wide)
+    ctx_move = exchange(chunk_count, send_ctx, got_ctx, 0, head_cols)
     pair_count = HEADS // 2
 
     def probabilities(queries, key_rows, bias, pairs):
@@ -624,7 +637,7 @@
                 pair_window(pair)[0],
                 dot_tn(block.astype(jnp.bfloat16), two_heads(v_time, pair)),
             )
-    send_ctx[...] = split(jnp.concatenate(ctx, axis=1))
+    send_ctx[...] = split(jnp.concatenate(ctx, axis=1)[:, :head_cols])
     ctx_move[0]()
     weight_ready(3)
     for low, high in cuts:
@@ -634,10 +647,10 @@
     turn(fold, fold_t)
     ctx_move[1]()
     block = merged(got_ctx).astype(jnp.bfloat16)
-    after_value = hidden[...] + dot_nn(block, out_time[...])
+    after_value = hidden[...] + dot_nn(block, out_time[:head_cols])
     after[...] = after_value
     inv_space = lax.rsqrt(jnp.mean(after_value * after_value, axis=-1, keepdims=True) + epsilon)
-    sums = add([base[:, low:high] for low, high in cuts], project(block, fold))
+    sums = add([base[:, low:high] for low, high in cuts], project(block, fold.at[:head_cols]))
     queries, key_rows, values = by_heads([inv_space * part for part in sums])
     values = jnp.concatenate([values, jnp.zeros((tokens, extra), jnp.bfloat16)], axis=1)
     parts = []
@@ -796,11 +809,12 @@
         vmem((tokens, wide), bf16),
         vmem((seq_count, rows, width), bf16),
         vmem((seq_count, rows, width), bf16),
-        vmem((seq_count, rows, wide), bf16),
-        vmem((seq_count, rows, wide), bf16),
+        vmem((seq_count, rows, head_cols), bf16),
+        vmem((seq_count, rows, head_cols), bf16),
         vmem((seq_count, rows, wide), bf16),
         vmem((seq_count, rows, wide), bf16),
         vmem((moves + 1, rows, width), bf16),
+        vmem((rows, head_cols), bf16),
         vmem((seq_count, rows, width), bf16),
         vmem((half_blocks, rows, width), bf16),
         vmem((half, width), bf16),
@@ -808,7 +822,6 @@
         dma((moves,)),
         dma((moves,)),
         dma((2,)),
-        dma((5,)),
         dma((5,)),
         dma((5,)),
         dma((1,)),

time: 35.9 us -> 35.9 us (level)
  no operation moved by 1% of the time
where the time goes in v5:
time: 35.9 us; the launch traced here: 35.8 us
  Pallas kernels  35 us (97%)
  local copies, waits for them, and re-layouts  0.72 us (2%)
    pallas_call x1, Pallas kernels, fused_device(): pl.pallas_call(functools.partial(fused_kernel, seq_count), out_shape=pltp...  35 us

profile of v5, /device:TPU:1, one launch (start us, length us, event | category | flops | bytes accessed | tf_op | source)
XLA Modules:
  0.0 35.8 jit_solution(16077765794579480476)
XLA Ops:
  0.0 35.0 %shard_map.109 = f32[64,1152]{1,0:T(8,128)S(1)} custom-call(bf16[128,1152]{1,0:T(8,128)(2,1)} %bitcast.8, bf16[128,1152]{1,0:T(8,128)(2,1)} %bitcast.9, bf16[128,1152]{1,0:T(8,128)(2,1)} %bitcast.10, f32[9,128]{1,0:T(8,128)} %bitcast.12, f32[9,128]{1,0:T(8,128)} %bitcast.13, f32[128,16]{1,0:T(8,128)} %bitcast.11, bf16[576,1728]{1,0:T(8,128)(2,1)} %proj_time_in.1, ...), custom_call_target="tpu_custom_call" | custom-call | tf_op jit(solution)/shard_map/pallas_call | solution.py:833
  35.0 0.7 %copy.13 = f32[1,64,1152]{2,1,0:T(8,128)} copy(f32[1,64,1152]{2,1,0:T(8,128)S(1)} %bitcast.7) | data formatting | bytes 589824
